TPU v7x, 128 devices: a whole 4x4x4 slice. The times are simulated.
128 devices in a mesh: aa: 8 (over y, core), ba: 16 (over x, z).
Axes of the slice: x: 4, y: 4, z: 4, core: 2. Of those that a mesh axis runs over, the one named last changes fastest.
Arguments:
- grid_nodes: bfloat16 [131072, 512], P(('aa', 'ba')), may hold values from -6 to 6
- mesh_nodes: bfloat16 [24576, 512], P(('aa', 'ba')), may hold values from -6 to 6
- owned_nodes: int32 [128], P(('aa', 'ba')), may hold values from 96 to 192, as said below
- grid_rim: int32 [128, 8, 128], P(('aa', 'ba')), may hold values from 0 to 1023
- mesh_rim: int32 [128, 8, 16], P(('aa', 'ba')), may hold values from 0 to 95
- long_send: int32 [128, 128, 8], P(('aa', 'ba')), may hold values from 0 to 15
- g2m_edges: int32 [128, 2, 3072], P(('aa', 'ba')), may hold values from 0 to 2047, as said below
- short_edges: int32 [128, 2, 1536], P(('aa', 'ba')), may hold values from 0 to 319, as said below
- long_edges: int32 [128, 2, 1536], P(('aa', 'ba')), may hold values from 0 to 1215, as said below
- m2g_edges: int32 [128, 3, 1024], P(('aa', 'ba')), may hold values from 0 to 319, as said below
- edge_first: bfloat16 [4, 2, 512, 512], replicated, may hold values from -0.1875 to 0.1875
- edge_second: bfloat16 [4, 512, 512], replicated, may hold values from -0.25 to 0.25
- edge_bias: float32 [4, 512], replicated, may hold values from -3 to 3
- edge_gain: float32 [4, 512], replicated, may hold values from 0.5 to 2
- node_first: bfloat16 [4, 2, 512, 512], replicated, may hold values from -0.1875 to 0.1875
- node_second: bfloat16 [4, 512, 512], replicated, may hold values from -0.25 to 0.25
- node_bias: float32 [4, 512], replicated, may hold values from -3 to 3
- node_gain: float32 [4, 512], replicated, may hold values from 0.5 to 2
Outputs:
- grid_out: bfloat16 [131072, 512], P(('aa', 'ba'))
- mesh_out: bfloat16 [24576, 512], P(('aa', 'ba'))
Inputs may be any that keep to these rules, and one draw needn't show every extreme that they name: `owned_nodes`: some device owns 192 nodes in every draw. `g2m_edges`: row 0 holds senders, row 1 receivers. On device d the first 16 * owned_nodes[d] slots are used, with receivers below owned_nodes[d]; the others have receiver 192. Senders at or above 1024 never name a direction with a_k = -1 on band i = 0 or a_k = 1 on band i = 7. `short_edges`: row 0 holds senders, row 1 receivers. On device d the first 8 * owned_nodes[d] slots are used, with receivers below owned_nodes[d]; the others have receiver 192. Senders below 192 are below owned_nodes[d]; senders at or above 192 never name a direction with a_k = -1 on band 0 or a_k = 1 on band 8 - 1. `long_edges`: row 0 holds senders, row 1 receivers. On device d the first 8 * owned_nodes[d] slots are used, with receivers below owned_nodes[d]; the others have receiver 192. Senders below 192 are below owned_nodes[d]. `m2g_edges`: senders below 192 are below owned_nodes[d]; senders at or above 192 never name a direction with a_k = -1 on band 0 or a_k = 1 on band 8 - 1.
All inputs are finite; a program needn't handle non-finite values.
Results may differ from a plain program's by a relative error of at most 0.013.
Values may be sent and summed in bfloat16 or wider, within the bound.
A program may use at most 128 MiB of HBM per device.

v0:
```python
import math

import jax
import jax.numpy as jnp
from jax import lax
from jax.sharding import PartitionSpec as P

EPSILON = 1e-05
RIM_PICKS = (0, 2, 4, 10, 14, 20, 22, 24)


def extended_2(value, sides, width):
    for axis, dim in sides:
        count, length = (lax.axis_size(axis), value.shape[dim])
        up = [(i, (i + 1) % count) for i in range(count)]
        down = [(j, i) for i, j in up]
        last = lax.slice_in_dim(value, length - width, length, axis=dim)
        initial = lax.slice_in_dim(value, 0, width, axis=dim)
        before = lax.ppermute(last, axis, up)
        after = lax.ppermute(initial, axis, down)
        value = jnp.concatenate([before, value, after], axis=dim)
    return value


def layer_norm(values, norm_gain):
    average = jnp.mean(values, axis=-1, keepdims=True)
    centred = values - average
    spread = jnp.mean(centred * centred, axis=-1, keepdims=True)
    return centred * lax.rsqrt(spread + EPSILON) * norm_gain


def pick_rows(table, row_ids):
    total = row_ids.shape[0]
    block = math.gcd(total, 512)
    blocked_ids = row_ids.reshape(total // block, block)
    table_rows = table.shape[0]

    def one_block(block_ids):
        member = block_ids[:, None] == lax.broadcasted_iota(jnp.int32, (block, table_rows), 1)
        if table.dtype == jnp.float32:
            return jnp.dot(
                member.astype(jnp.float32),
                table,
                precision=lax.Precision.HIGHEST,
                preferred_element_type=jnp.float32,
            )
        return jnp.dot(
            member.astype(table.dtype), table, preferred_element_type=jnp.float32
        ).astype(table.dtype)

    picked = lax.map(one_block, blocked_ids)
    return picked.reshape(total, table.shape[1])


def rim_blocks(projected, rim_rows):
    feature_count = projected.shape[1]
    block_depth = rim_rows.shape[1]
    picked = pick_rows(projected, rim_rows.reshape(-1)).reshape(8, block_depth, feature_count)
    centre = jnp.zeros((1, block_depth, feature_count), projected.dtype)
    stacked = jnp.concatenate([picked[:4], centre, picked[4:]], 0)
    return stacked.reshape(3, 3, block_depth, feature_count)


def rim_sources(extended):
    flattened = extended.reshape((25,) + extended.shape[2:])
    chosen = [flattened[position] for position in RIM_PICKS]
    return jnp.concatenate(chosen, 0)


def messages(gathered, target_proj, biases, second, norm_gain):
    hidden = jax.nn.silu(gathered.astype(jnp.float32) + target_proj + biases).astype(jnp.bfloat16)
    result = jnp.dot(hidden, second, preferred_element_type=jnp.float32)
    return layer_norm(result, norm_gain).astype(jnp.bfloat16)


def node_update(node_rows, totals, first_layer, biases, second, norm_gain):
    summed_input = jnp.dot(node_rows, first_layer[0], preferred_element_type=jnp.float32)
    summed_input = (
        summed_input
        + jnp.dot(totals.astype(jnp.bfloat16), first_layer[1], preferred_element_type=jnp.float32)
        + biases
    )
    hidden = jax.nn.silu(summed_input).astype(jnp.bfloat16)
    result = jnp.dot(hidden, second, preferred_element_type=jnp.float32)
    return (node_rows.astype(jnp.float32) + layer_norm(result, norm_gain)).astype(jnp.bfloat16)


def mesh_round(source_table, node_rows, edge_list, weights, section_index):
    edge_first, edge_second, edge_bias, edge_gain, node_first, node_second, node_bias, node_gain = (
        weights
    )
    senders = edge_list[0, 0]
    targets = edge_list[0, 1]
    slot_count = node_rows.shape[0]
    target_proj = jnp.dot(
        node_rows, edge_first[section_index, 1], preferred_element_type=jnp.float32
    )
    picked = pick_rows(target_proj, jnp.minimum(targets, slot_count - 1))
    gathered = pick_rows(source_table, senders)
    message_rows = messages(
        gathered,
        picked,
        edge_bias[section_index],
        edge_second[section_index],
        edge_gain[section_index],
    )
    member = lax.broadcasted_iota(jnp.int32, (slot_count, targets.shape[0]), 0) == targets[None, :]
    totals = jnp.dot(member.astype(jnp.bfloat16), message_rows, preferred_element_type=jnp.float32)
    return node_update(
        node_rows,
        totals,
        node_first[section_index],
        node_bias[section_index],
        node_second[section_index],
        node_gain[section_index],
    )


def per_device(
    grid_nodes,
    mesh_nodes,
    owned_nodes,
    grid_rim,
    mesh_rim,
    long_send,
    g2m_edges,
    short_edges,
    long_edges,
    m2g_edges,
    edge_first,
    edge_second,
    edge_bias,
    edge_gain,
    node_first,
    node_second,
    node_bias,
    node_gain,
):
    weights = (
        edge_first,
        edge_second,
        edge_bias,
        edge_gain,
        node_first,
        node_second,
        node_bias,
        node_gain,
    )
    grid_proj = jnp.dot(grid_nodes, edge_first[0, 0], preferred_element_type=jnp.float32).astype(
        jnp.bfloat16
    )
    grid_extended = extended_2(rim_blocks(grid_proj, grid_rim[0]), (("aa", 0), ("ba", 1)), 1)
    source_table = jnp.concatenate([grid_proj, rim_sources(grid_extended)], 0)
    mesh_one = mesh_round(source_table, mesh_nodes, g2m_edges, weights, 0)
    short_proj = jnp.dot(mesh_one, edge_first[1, 0], preferred_element_type=jnp.float32).astype(
        jnp.bfloat16
    )
    short_extended = extended_2(rim_blocks(short_proj, mesh_rim[0]), (("aa", 0), ("ba", 1)), 1)
    source_table = jnp.concatenate([short_proj, rim_sources(short_extended)], 0)
    mesh_two = mesh_round(source_table, mesh_one, short_edges, weights, 1)
    long_proj = jnp.dot(mesh_two, edge_first[2, 0], preferred_element_type=jnp.float32).astype(
        jnp.bfloat16
    )
    send_lists = long_send[0]
    peer_count = send_lists.shape[0]
    list_depth = send_lists.shape[1]
    feature_count = long_proj.shape[1]
    outgoing = pick_rows(long_proj, send_lists.reshape(-1)).reshape(
        peer_count, list_depth, feature_count
    )
    incoming = lax.all_to_all(outgoing, ("aa", "ba"), split_axis=0, concat_axis=0, tiled=True)
    incoming = incoming.reshape(peer_count * list_depth, feature_count)
    source_table = jnp.concatenate([long_proj, incoming], 0)
    mesh_three = mesh_round(source_table, mesh_two, long_edges, weights, 2)
    decode_proj = jnp.dot(mesh_three, edge_first[3, 0], preferred_element_type=jnp.float32).astype(
        jnp.bfloat16
    )
    decode_extended = extended_2(rim_blocks(decode_proj, mesh_rim[0]), (("aa", 0), ("ba", 1)), 1)
    source_table = jnp.concatenate([decode_proj, rim_sources(decode_extended)], 0)
    grid_target = jnp.dot(grid_nodes, edge_first[3, 1], preferred_element_type=jnp.float32)
    grid_count = grid_nodes.shape[0]
    gathered = pick_rows(source_table, m2g_edges[0].reshape(-1))
    repeated = jnp.concatenate([grid_target, grid_target, grid_target], 0)
    message_rows = messages(gathered, repeated, edge_bias[3], edge_second[3], edge_gain[3])
    message_rows = message_rows.reshape(3, grid_count, feature_count)
    totals = jnp.sum(message_rows.astype(jnp.float32), axis=0)
    grid_out = node_update(
        grid_nodes, totals, node_first[3], node_bias[3], node_second[3], node_gain[3]
    )
    alive_rows = lax.broadcasted_iota(jnp.int32, (mesh_three.shape[0], 1), 0) < owned_nodes[0]
    mesh_out = jnp.where(alive_rows, mesh_three, jnp.zeros_like(mesh_three))
    return (grid_out, mesh_out)


def solution(mesh):
    in_specs = (
        P(("aa", "ba"), None),
        P(("aa", "ba"), None),
        P(("aa", "ba")),
        P(("aa", "ba"), None, None),
        P(("aa", "ba"), None, None),
        P(("aa", "ba"), None, None),
        P(("aa", "ba"), None, None),
        P(("aa", "ba"), None, None),
        P(("aa", "ba"), None, None),
        P(("aa", "ba"), None, None),
        P(),
        P(),
        P(),
        P(),
        P(),
        P(),
        P(),
        P(),
    )
    out_specs = (P(("aa", "ba"), None), P(("aa", "ba"), None))
    return jax.shard_map(
        per_device, mesh=mesh, in_specs=in_specs, out_specs=out_specs, check_vma=False
    )
```

profile of v0, /device:TPU:0, one launch (start us, length us, event | category | flops | bytes accessed | tf_op | source)
XLA Modules:
  0.0 245.7 jit_solution(11675926862094378936)
XLA Ops:
  1.3 3.1 %constant_dynamic-update-slice_fusion = (bf16[2048,512]{1,0:T(8,128)(2,1)}, bf16[1024,512]{1,0:T(8,128)(2,1)S(1)}) fusion(bf16[1024,512]{1,0:T(8,128)(2,1)} %param.36, bf16[4,2,512,512]{3,2,1,0:T(8,128)(2,1)} %param.46), kind=kOutput, calls=%fused_computation.211 | convolution fusion | flops 537395200 | bytes 3670016 | tf_op jit(solution)/shard_map/dot_general | solution.py:149
  12.1 9.9 %while.100 = (s32[]{:T(128)}, f32[6,512,512]{2,1,0:T(8,128)}, s32[6,512]{1,0:T(8,128)S(1)}, f32[192,512]{1,0:T(8,128)S(1)}, s32[]{:T(128)}) while((s32[]{:T(128)}, f32[6,512,512]{2,1,0:T(8,128)}, s32[6,512]{1,0:T(8,128)S(1)}, f32[192,512]{1,0:T(8,128)S(1)}, s32[]{:T(128)}) %tuple.171), condition=%wide.region_5.6_spmd, body=%wide.region_4.5_spmd.sunk | while | flops 604078080 | bytes 1448513 | solution.py:51
  34.1 4.3 %collective-permute-start.3 = (bf16[5,1,128,512]{3,2,1,0:T(8,128)(2,1)}, bf16[5,1,128,512]{3,2,1,0:T(8,128)(2,1)}, u32[]{:S(2)}, u32[]{:S(2)}) collective-permute-start(bf16[5,1,128,512]{3,2,1,0:T(8,128)(2,1)} %get-tuple-element.320), channel_id=1, source_target_pairs={{1,0},{2,1},{3,2},{4,3},{5,4},{6,5},{7,6},{8,7},{9,8},{10,9},{11,1... | collective-permute-start | bytes 1966088 | tf_op jit(solution)/shard_map/ppermute | solution.py:20
  44.9 3.5 %pad_maximum_fusion = f32[3072,512]{1,0:T(8,128)} fusion(f32[1024,512]{1,0:T(8,128)S(1)} %fusion.58), kind=kLoop, calls=%fused_computation.54 | loop fusion | flops 3145728 | bytes 8388608 | tf_op jit(solution)/shard_map/concatenate | solution.py:183
  48.4 3.9 %collective-permute-done.2 = bf16[5,1,128,512]{3,2,1,0:T(8,128)(2,1)} collective-permute-done((bf16[5,1,128,512]{3,2,1,0:T(8,128)(2,1)}, bf16[5,1,128,512]{3,2,1,0:T(8,128)(2,1)}, u32[]{:S(2)}, u32[]{:S(2)}) %collective-permute-start.2) | collective-permute-done | bytes 655392 | tf_op jit(solution)/shard_map/ppermute | solution.py:19
  59.8 21.8 %while.99 = (s32[]{:T(128)}, bf16[6,512,512]{2,1,0:T(8,128)(2,1)S(1)}, s32[6,512]{1,0:T(8,128)}, bf16[2048,512]{1,0:T(8,128)(2,1)}, s32[]{:T(128)}) while((s32[]{:T(128)}, bf16[6,512,512]{2,1,0:T(8,128)(2,1)S(1)}, s32[6,512]{1,0:T(8,128)}, bf16[2048,512]{1,0:T(8,128)(2,1)}, s32[]{:T(128)}) %tuple.177), condition=%wide.region_3.4_spmd, body=%wide.region_2.3_spmd.sunk | while | flops 1075052544 | bytes 2627653 | solution.py:51
  81.6 3.8 %multiply_convert_fusion.3 = bf16[6,512,512]{2,1,0:T(8,128)(2,1)S(1)} fusion(f32[6,512,512]{2,1,0:T(8,128)} %get-tuple-element.226, bf16[6,512,512]{2,1,0:T(8,128)(2,1)S(1)} %get-tuple-element.225, f32[512]{0:T(512)S(1)} %bitcast.438), kind=kLoop, calls=%fused_computation.60 | loop fusion | flops 12582912 | bytes 12584960 | tf_op jit(solution)/shard_map/convert_element_type | solution.py:71
  85.4 3.0 %fusion.145 = (f32[3072]{0:T(1024)S(1)}, f32[3072,512]{0,1:T(8,128)S(1)}) fusion(bf16[3072,512]{1,0:T(8,128)(2,1)S(1)} %bitcast.377, bf16[4,512,512]{2,1,0:T(8,128)(2,1)} %param.47), kind=kOutput, calls=%fused_computation.282 | convolution fusion | flops 1612182528 | bytes 9973760 | tf_op jit(solution)/shard_map/dot_general | solution.py:72
  91.1 4.5 %multiply_convert_fusion.30 = bf16[192,512]{1,0:T(8,128)(2,1)S(1)} fusion(f32[192,512]{1,0:T(8,128)S(1)} %copy-done.9, bf16[4,2,512,512]{3,2,1,0:T(8,128)(2,1)} %param.50, f32[3072,512]{0,1:T(8,128)} %copy-done, f32[512]{0:T(512)S(1)} %bitcast.444, f32[3072]{0:T(1024)S(1)} %add_rsqrt_fusion.1, f32[3072]{0:T(1024)S(1)} %broadcast_multiply_fusion.1, ...), kind=kOutput, calls=%fused_computation.182 | convolution fusion | flops 712310784 | bytes 7446528 | tf_op jit(solution)/shard_map/dot_general | solution.py:80
  105.6 4.1 %while.102 = (s32[]{:T(128)}, f32[3,512,512]{2,1,0:T(8,128)S(1)}, s32[3,512]{1,0:T(4,128)}, f32[192,512]{1,0:T(8,128)S(1)}, s32[]{:T(128)}) while((s32[]{:T(128)}, f32[3,512,512]{2,1,0:T(8,128)S(1)}, s32[3,512]{1,0:T(4,128)}, f32[192,512]{1,0:T(8,128)S(1)}, s32[]{:T(128)}) %tuple.180), condition=%wide.region_13.14_spmd, body=%wide.region_12.13_spmd.sunk | while | flops 604078080 | bytes 1448005 | solution.py:51
  111.6 5.3 %collective-permute-start.7 = (bf16[5,1,16,512]{3,2,1,0:T(8,128)(2,1)S(1)}, bf16[5,1,16,512]{3,2,1,0:T(8,128)(2,1)S(1)}, u32[]{:S(2)}, u32[]{:S(2)}) collective-permute-start(bf16[5,1,16,512]{3,2,1,0:T(8,128)(2,1)S(1)} %get-tuple-element.328), channel_id=1, source_target_pairs={{1,0},{2,1},{3,2},{4,3},{5,4},{6,5},{7,6},{8,7},{9,8},{10,9},{11,1... | collective-permute-start | bytes 245768 | tf_op jit(solution)/shard_map/ppermute | solution.py:20
  126.3 8.9 %while.101 = (s32[]{:T(128)}, bf16[3,512,512]{2,1,0:T(8,128)(2,1)}, s32[3,512]{1,0:T(4,128)}, bf16[320,512]{1,0:T(8,128)(2,1)}, s32[]{:T(128)}) while((s32[]{:T(128)}, bf16[3,512,512]{2,1,0:T(8,128)(2,1)}, s32[3,512]{1,0:T(4,128)}, bf16[320,512]{1,0:T(8,128)(2,1)}, s32[]{:T(128)}) %tuple.183), condition=%wide.region_11.12_spmd, body=%wide.region_10.11_spmd.sunk | while | flops 168198144 | bytes 858689 | solution.py:51
  154.2 9.0 %all-to-all-start = ((bf16[128,8,512]{2,1,0:T(8,128)(2,1)}), bf16[128,8,512]{2,1,0:T(8,128)(2,1)}, u32[]{:S(2)}, u32[]{:S(2)}) async-start(bf16[128,8,512]{2,1,0:T(8,128)(2,1)} %bitcast.72), calls=%async_computation | async-start | bytes 2097152 | tf_op jit(solution)/shard_map/all_to_all | solution.py:171
  163.6 4.1 %while.105 = (s32[]{:T(128)}, f32[3,512,512]{2,1,0:T(8,128)S(1)}, s32[3,512]{1,0:T(4,128)}, f32[192,512]{1,0:T(8,128)S(1)}, s32[]{:T(128)}) while((s32[]{:T(128)}, f32[3,512,512]{2,1,0:T(8,128)S(1)}, s32[3,512]{1,0:T(4,128)}, f32[192,512]{1,0:T(8,128)S(1)}, s32[]{:T(128)}) %tuple.186), condition=%wide.region_23.24_spmd, body=%wide.region_22.23_spmd.sunk | while | flops 604078080 | bytes 1448005 | solution.py:51
  167.6 14.1 %all-to-all-done = bf16[128,8,512]{2,1,0:T(8,128)(2,1)} async-done(((bf16[128,8,512]{2,1,0:T(8,128)(2,1)}), bf16[128,8,512]{2,1,0:T(8,128)(2,1)}, u32[]{:S(2)}, u32[]{:S(2)}) %all-to-all-start) | async-done | bytes 1048608 | tf_op jit(solution)/shard_map/all_to_all | solution.py:171
  185.5 9.0 %while.104 = (s32[]{:T(128)}, bf16[3,512,512]{2,1,0:T(8,128)(2,1)}, s32[3,512]{1,0:T(4,128)S(1)}, bf16[1216,512]{1,0:T(8,128)(2,1)}, s32[]{:T(128)}) while((s32[]{:T(128)}, bf16[3,512,512]{2,1,0:T(8,128)(2,1)}, s32[3,512]{1,0:T(4,128)S(1)}, bf16[1216,512]{1,0:T(8,128)(2,1)}, s32[]{:T(128)}) %tuple.192), condition=%wide.region_21.22_spmd, body=%wide.region_20.21_spmd.sunk | while | flops 638418944 | bytes 1776193 | solution.py:51
  185.5 3.0 %fusion.217 = bf16[3,512,512]{2,1,0:T(8,128)(2,1)} fusion(bf16[3,512,512]{2,1,0:T(8,128)(2,1)} %get-tuple-element.712, s32[]{:T(128)} %get-tuple-element.711, bf16[1216,512]{1,0:T(8,128)(2,1)} %get-tuple-element.719, s32[512]{0:T(512)S(1)} %bitcast.425), kind=kOutput, calls=%fused_computation.41.clone.1 | convolution fusion | flops 638418944 | bytes 1772032 | tf_op jit(solution)/shard_map/while/body/eval_jaxpr/dot_general | solution.py:47
  188.5 3.0 %fusion.217 = bf16[3,512,512]{2,1,0:T(8,128)(2,1)} fusion(bf16[3,512,512]{2,1,0:T(8,128)(2,1)} %get-tuple-element.712, s32[]{:T(128)} %get-tuple-element.711, bf16[1216,512]{1,0:T(8,128)(2,1)} %get-tuple-element.719, s32[512]{0:T(512)S(1)} %bitcast.425), kind=kOutput, calls=%fused_computation.41.clone.1 | convolution fusion | flops 638418944 | bytes 1772032 | tf_op jit(solution)/shard_map/while/body/eval_jaxpr/dot_general | solution.py:47
  191.5 3.0 %fusion.217 = bf16[3,512,512]{2,1,0:T(8,128)(2,1)} fusion(bf16[3,512,512]{2,1,0:T(8,128)(2,1)} %get-tuple-element.712, s32[]{:T(128)} %get-tuple-element.711, bf16[1216,512]{1,0:T(8,128)(2,1)} %get-tuple-element.719, s32[512]{0:T(512)S(1)} %bitcast.425), kind=kOutput, calls=%fused_computation.41.clone.1 | convolution fusion | flops 638418944 | bytes 1772032 | tf_op jit(solution)/shard_map/while/body/eval_jaxpr/dot_general | solution.py:47
  213.0 4.4 %collective-permute-start.11 = (bf16[5,1,16,512]{3,2,1,0:T(8,128)(2,1)S(1)}, bf16[5,1,16,512]{3,2,1,0:T(8,128)(2,1)S(1)}, u32[]{:S(2)}, u32[]{:S(2)}) collective-permute-start(bf16[5,1,16,512]{3,2,1,0:T(8,128)(2,1)S(1)} %get-tuple-element.326), channel_id=1, source_target_pairs={{1,0},{2,1},{3,2},{4,3},{5,4},{6,5},{7,6},{8,7},{9,8},{10,9},{11,1... | collective-permute-start | bytes 245768 | tf_op jit(solution)/shard_map/ppermute | solution.py:20
  217.5 3.1 %fusion.91 = f32[1024,512]{1,0:T(8,128)} fusion(bf16[1024,512]{1,0:T(8,128)(2,1)S(1)} %copy-done.2, bf16[4,2,512,512]{3,2,1,0:T(8,128)(2,1)} %param.50), kind=kOutput, calls=%fused_computation.146 | convolution fusion | flops 536870912 | bytes 3670016 | tf_op jit(solution)/shard_map/dot_general | solution.py:77
  222.4 3.1 %while.106 = (s32[]{:T(128)}, bf16[6,512,512]{2,1,0:T(8,128)(2,1)S(1)}, s32[6,512]{1,0:T(8,128)S(1)}, bf16[320,512]{1,0:T(8,128)(2,1)S(1)}, s32[]{:T(128)}) while((s32[]{:T(128)}, bf16[6,512,512]{2,1,0:T(8,128)(2,1)S(1)}, s32[6,512]{1,0:T(8,128)S(1)}, bf16[320,512]{1,0:T(8,128)(2,1)S(1)}, s32[]{:T(128)}) %tuple.195), condition=%wide.region_29.30_spmd, body=%wide.region_28.29_spmd.sunk | while | flops 168198144 | bytes 858181 | solution.py:51
  225.6 3.8 %multiply_convert_fusion.1 = bf16[6,512,512]{2,1,0:T(8,128)(2,1)S(1)} fusion(f32[6,512,512]{2,1,0:T(8,128)} %bitcast.376, bf16[6,512,512]{2,1,0:T(8,128)(2,1)S(1)} %get-tuple-element.232, f32[512]{0:T(512)S(1)} %bitcast.437), kind=kLoop, calls=%fused_computation.57 | loop fusion | flops 12582912 | bytes 12584960 | tf_op jit(solution)/shard_map/convert_element_type | solution.py:71
  237.9 3.8 %fusion.152 = (f32[1024]{0:T(1024)S(1)}, f32[1024,512]{0,1:T(8,128)S(1)}) fusion(bf16[4,512,512]{2,1,0:T(8,128)(2,1)} %param.51, f32[1024,512]{1,0:T(8,128)} %fusion.91, bf16[1024,512]{1,0:T(8,128)(2,1)} %reduce_sum.170, f32[512]{0:T(512)S(1)} %bitcast.439, bf16[4,2,512,512]{3,2,1,0:T(8,128)(2,1)} %param.50), kind=kOutput, calls=%fused_computation.289 | convolution fusion | flops 1077935104 | bytes 6297600 | tf_op jit(solution)/shard_map/dot_general | solution.py:84
  (285 shorter events, 168.2 us)
Async XLA Ops:
  7.1 22.6 %collective-permute-start = (bf16[1,3,128,512]{3,2,1,0:T(8,128)(2,1)}, bf16[1,3,128,512]{3,2,1,0:T(8,128)(2,1)}, u32[]{:S(2)}, u32[]{:S(2)}) collective-permute-start(bf16[1,3,128,512]{3,2,1,0:T(8,128)(2,1)} %bitcast.22), channel_id=1, source_target_pairs={{0,16},{16,32},{32,48},{48,64},{64,80},{80,96},{96,112},{112,0},{1... | collective-permute-start | bytes 1179656 | tf_op jit(solution)/shard_map/ppermute | solution.py:19
  7.1 22.6 %collective-permute-start.1 = (bf16[1,3,128,512]{3,2,1,0:T(8,128)(2,1)}, bf16[1,3,128,512]{3,2,1,0:T(8,128)(2,1)}, u32[]{:S(2)}, u32[]{:S(2)}) collective-permute-start(bf16[1,3,128,512]{3,2,1,0:T(8,128)(2,1)} %bitcast.26), channel_id=1, source_target_pairs={{16,0},{32,16},{48,32},{64,48},{80,64},{96,80},{112,96},{0,112},{1... | collective-permute-start | bytes 1179656 | tf_op jit(solution)/shard_map/ppermute | solution.py:20
  12.1 9.9 %copy-start.22 = (f32[4,512]{1,0:T(4,128)S(1)}, f32[4,512]{1,0:T(4,128)}, u32[]{:S(2)}) copy-start(f32[4,512]{1,0:T(4,128)} %param.48) | copy-start | bytes 24580
  12.1 10.5 %copy-start.23 = (f32[4,512]{1,0:T(4,128)S(1)}, f32[4,512]{1,0:T(4,128)}, u32[]{:S(2)}) copy-start(f32[4,512]{1,0:T(4,128)} %param.49) | copy-start | bytes 24580
  12.1 11.1 %copy-start.24 = (f32[4,512]{1,0:T(4,128)S(1)}, f32[4,512]{1,0:T(4,128)}, u32[]{:S(2)}) copy-start(f32[4,512]{1,0:T(4,128)} %param.52) | copy-start | bytes 24580
  12.1 13.8 %copy-start.25 = (f32[4,512]{1,0:T(4,128)S(1)}, f32[4,512]{1,0:T(4,128)}, u32[]{:S(2)}) copy-start(f32[4,512]{1,0:T(4,128)} %param.53) | copy-start | bytes 24580
  27.9 10.5 %copy-start.15 = (s32[1,2,1536]{2,1,0:T(2,128)S(1)}, s32[1,2,1536]{2,1,0:T(2,128)}, u32[]{:S(2)}) copy-start(s32[1,2,1536]{2,1,0:T(2,128)} %param.44) | copy-start | bytes 36868
  27.9 11.7 %copy-start.33 = (s32[1,8,16]{2,1,0:T(8,128)S(1)}, s32[1,8,16]{2,1,0:T(8,128)}, u32[]{:S(2)}) copy-start(s32[1,8,16]{2,1,0:T(8,128)} %param.40) | copy-start | bytes 1540
  27.9 13.6 %copy-start.32 = (s32[1,128,8]{1,2,0:T(8,128)S(1)}, s32[1,128,8]{1,2,0:T(8,128)}, u32[]{:S(2)}) copy-start(s32[1,128,8]{1,2,0:T(8,128)} %param.41) | copy-start | bytes 12292
  32.0 20.3 %collective-permute-start.2 = (bf16[5,1,128,512]{3,2,1,0:T(8,128)(2,1)}, bf16[5,1,128,512]{3,2,1,0:T(8,128)(2,1)}, u32[]{:S(2)}, u32[]{:S(2)}) collective-permute-start(bf16[5,1,128,512]{3,2,1,0:T(8,128)(2,1)} %get-tuple-element.319), channel_id=1, source_target_pairs={{0,1},{1,2},{2,3},{3,4},{4,5},{5,6},{6,7},{7,8},{8,9},{9,10},{10,1... | collective-permute-start | bytes 1966088 | tf_op jit(solution)/shard_map/ppermute | solution.py:19
  34.1 18.3 %collective-permute-start.3 = (bf16[5,1,128,512]{3,2,1,0:T(8,128)(2,1)}, bf16[5,1,128,512]{3,2,1,0:T(8,128)(2,1)}, u32[]{:S(2)}, u32[]{:S(2)}) collective-permute-start(bf16[5,1,128,512]{3,2,1,0:T(8,128)(2,1)} %get-tuple-element.320), channel_id=1, source_target_pairs={{1,0},{2,1},{3,2},{4,3},{5,4},{6,5},{7,6},{8,7},{9,8},{10,9},{11,1... | collective-permute-start | bytes 1966088 | tf_op jit(solution)/shard_map/ppermute | solution.py:20
  59.8 21.8 %copy-start.27 = (f32[1,512]{1,0:T(1,128)S(1)}, f32[1,512]{1,0:T(1,128)}, u32[]{:S(2)}) copy-start(f32[1,512]{1,0:T(1,128)} %get-tuple-element.352) | copy-start | bytes 6148
  102.3 8.4 %collective-permute-start.4 = (bf16[1,3,16,512]{3,2,1,0:T(8,128)(2,1)}, bf16[1,3,16,512]{3,2,1,0:T(8,128)(2,1)}, u32[]{:S(2)}, u32[]{:S(2)}) collective-permute-start(bf16[1,3,16,512]{3,2,1,0:T(8,128)(2,1)} %bitcast.47), channel_id=1, source_target_pairs={{0,16},{16,32},{32,48},{48,64},{64,80},{80,96},{96,112},{112,0},{1... | collective-permute-start | bytes 147464 | tf_op jit(solution)/shard_map/ppermute | solution.py:19
  102.3 8.4 %collective-permute-start.5 = (bf16[1,3,16,512]{3,2,1,0:T(8,128)(2,1)}, bf16[1,3,16,512]{3,2,1,0:T(8,128)(2,1)}, u32[]{:S(2)}, u32[]{:S(2)}) collective-permute-start(bf16[1,3,16,512]{3,2,1,0:T(8,128)(2,1)} %bitcast.51), channel_id=1, source_target_pairs={{16,0},{32,16},{48,32},{64,48},{80,64},{96,80},{112,96},{0,112},{1... | collective-permute-start | bytes 147464 | tf_op jit(solution)/shard_map/ppermute | solution.py:20
  111.5 7.8 %collective-permute-start.6 = (bf16[5,1,16,512]{3,2,1,0:T(8,128)(2,1)S(1)}, bf16[5,1,16,512]{3,2,1,0:T(8,128)(2,1)S(1)}, u32[]{:S(2)}, u32[]{:S(2)}) collective-permute-start(bf16[5,1,16,512]{3,2,1,0:T(8,128)(2,1)S(1)} %get-tuple-element.327), channel_id=1, source_target_pairs={{0,1},{1,2},{2,3},{3,4},{4,5},{5,6},{6,7},{7,8},{8,9},{9,10},{10,1... | collective-permute-start | bytes 245768 | tf_op jit(solution)/shard_map/ppermute | solution.py:19
  111.6 7.8 %collective-permute-start.7 = (bf16[5,1,16,512]{3,2,1,0:T(8,128)(2,1)S(1)}, bf16[5,1,16,512]{3,2,1,0:T(8,128)(2,1)S(1)}, u32[]{:S(2)}, u32[]{:S(2)}) collective-permute-start(bf16[5,1,16,512]{3,2,1,0:T(8,128)(2,1)S(1)} %get-tuple-element.328), channel_id=1, source_target_pairs={{1,0},{2,1},{3,2},{4,3},{5,4},{6,5},{7,6},{8,7},{9,8},{10,9},{11,1... | collective-permute-start | bytes 245768 | tf_op jit(solution)/shard_map/ppermute | solution.py:20
  154.2 27.6 %all-to-all-start = ((bf16[128,8,512]{2,1,0:T(8,128)(2,1)}), bf16[128,8,512]{2,1,0:T(8,128)(2,1)}, u32[]{:S(2)}, u32[]{:S(2)}) async-start(bf16[128,8,512]{2,1,0:T(8,128)(2,1)} %bitcast.72), calls=%async_computation | async-start | bytes 2097152 | tf_op jit(solution)/shard_map/all_to_all | solution.py:171
  185.5 9.0 %copy-start.19 = (f32[1,512]{1,0:T(1,128)S(1)}, f32[1,512]{1,0:T(1,128)}, u32[]{:S(2)}) copy-start(f32[1,512]{1,0:T(1,128)} %get-tuple-element.353) | copy-start | bytes 6148
  202.2 15.3 %copy-start.2 = (bf16[1024,512]{1,0:T(8,128)(2,1)S(1)}, bf16[1024,512]{1,0:T(8,128)(2,1)}, u32[]{:S(2)}) copy-start(bf16[1024,512]{1,0:T(8,128)(2,1)} %param.36) | copy-start | bytes 3145732
  207.0 4.7 %collective-permute-start.8 = (bf16[1,3,16,512]{3,2,1,0:T(8,128)(2,1)S(1)}, bf16[1,3,16,512]{3,2,1,0:T(8,128)(2,1)S(1)}, u32[]{:S(2)}, u32[]{:S(2)}) collective-permute-start(bf16[1,3,16,512]{3,2,1,0:T(8,128)(2,1)S(1)} %bitcast.428), channel_id=1, source_target_pairs={{0,16},{16,32},{32,48},{48,64},{64,80},{80,96},{96,112},{112,0},{1... | collective-permute-start | bytes 147464 | tf_op jit(solution)/shard_map/ppermute | solution.py:19
  207.0 4.7 %collective-permute-start.9 = (bf16[1,3,16,512]{3,2,1,0:T(8,128)(2,1)S(1)}, bf16[1,3,16,512]{3,2,1,0:T(8,128)(2,1)S(1)}, u32[]{:S(2)}, u32[]{:S(2)}) collective-permute-start(bf16[1,3,16,512]{3,2,1,0:T(8,128)(2,1)S(1)} %bitcast.427), channel_id=1, source_target_pairs={{16,0},{32,16},{48,32},{64,48},{80,64},{96,80},{112,96},{0,112},{1... | collective-permute-start | bytes 147464 | tf_op jit(solution)/shard_map/ppermute | solution.py:20
  210.1 11.8 %copy-start.13 = (s32[1,3,1024]{2,0,1:T(1,128)S(1)}, s32[1,3,1024]{2,0,1:T(1,128)}, u32[]{:S(2)}) copy-start(s32[1,3,1024]{2,0,1:T(1,128)} %param.45) | copy-start | bytes 36868
  211.8 10.1 %collective-permute-start.10 = (bf16[5,1,16,512]{3,2,1,0:T(8,128)(2,1)S(1)}, bf16[5,1,16,512]{3,2,1,0:T(8,128)(2,1)S(1)}, u32[]{:S(2)}, u32[]{:S(2)}) collective-permute-start(bf16[5,1,16,512]{3,2,1,0:T(8,128)(2,1)S(1)} %get-tuple-element.325), channel_id=1, source_target_pairs={{0,1},{1,2},{2,3},{3,4},{4,5},{5,6},{6,7},{7,8},{8,9},{9,10},{10,1... | collective-permute-start | bytes 245768 | tf_op jit(solution)/shard_map/ppermute | solution.py:19
  213.0 8.9 %collective-permute-start.11 = (bf16[5,1,16,512]{3,2,1,0:T(8,128)(2,1)S(1)}, bf16[5,1,16,512]{3,2,1,0:T(8,128)(2,1)S(1)}, u32[]{:S(2)}, u32[]{:S(2)}) collective-permute-start(bf16[5,1,16,512]{3,2,1,0:T(8,128)(2,1)S(1)} %get-tuple-element.326), channel_id=1, source_target_pairs={{1,0},{2,1},{3,2},{4,3},{5,4},{6,5},{7,6},{8,7},{9,8},{10,9},{11,1... | collective-permute-start | bytes 245768 | tf_op jit(solution)/shard_map/ppermute | solution.py:20
  (26 other events, 97.3 us)
where the time goes:
time: 248 us; the launch traced here: 246 us
  matrix products  104 us (42%)
  local copies, waits for them, and re-layouts  43 us (17%)
  other arithmetic  41 us (17%)
  starting transfers between devices  35.3 us (14%)
  waiting for transfers between devices  20 us (8%)
    dot_general x24, matrix products, one_block(): jnp.dot(member.astype(table.dtype), table, preferred_element_type=jnp.flo...  40.2 us
    ppermute x6, starting transfers between devices, extended_2(): after = lax.ppermute(initial, axis, down)  22.9 us
    unnamed x98, local copies, waits for them, and re-layouts  15.8 us
    all_to_all x1, waiting for transfers between devices, per_device(): lax.all_to_all(outgoing, ('aa', 'ba'), split_axis=0, concat_axis=0, tiled...  14.1 us
    dot_general x12, matrix products, one_block(): jnp.dot(member.astype(jnp.float32), table, precision=lax.Precision.HIGHES...  13.5 us
    convert_element_type x4, other arithmetic, messages(): jax.nn.silu(gathered.astype(jnp.float32) + target_proj + biases)  12.2 us
    dynamic_slice x34, local copies, waits for them, and re-layouts, pick_rows(): picked = lax.map(one_block, blocked_ids)  10.8 us
    dot_general x4, matrix products, messages(): result = jnp.dot(hidden, second, preferred_element_type=jnp.float32)  10.1 us
  transfers between devices with their start and end apart: 13, of which 4 were waited for; matrix products, arithmetic and copies ran while one was open for 18% of the time, Pallas kernels for 0%

commit v1 on v0

v1 whole, which is shorter than its diff:
```python
import functools

import jax
import jax.numpy as jnp
from jax import lax
from jax.experimental import pallas as pl
from jax.experimental.pallas import tpu as pltpu
from jax.sharding import PartitionSpec as P

EPSILON = 1e-05
D = 512
G_DEV = 1024
M_DEV = 192
GB = 128
HB = 16
KL = 8
N_AA = 8
N_BA = 16
DEVICES = 128
E_G2M = 3072
E_MESH = 1536
TILE = 512
ALONG_FIRST = (-1, -1, -1, 0, 0, 1, 1, 1)
ALONG_SECOND = (-1, 0, 1, -1, 1, -1, 0, 1)
F32 = jnp.float32
BF16 = jnp.bfloat16
MESH = pl.DeviceIdType.MESH


def dot(a, b):
    return jnp.dot(a, b, preferred_element_type=F32)


def silu(x):
    half = 0.5 * x
    return half * jnp.tanh(half) + half


def normalised(values):
    centred = values - jnp.mean(values, axis=-1, keepdims=True)
    spread = jnp.mean(centred * centred, axis=-1, keepdims=True)
    return centred * lax.rsqrt(spread + EPSILON)


def columns(row):
    parts = []
    for start in range(0, row.shape[1], 128):
        part = row[:, start : start + 128].astype(F32)
        parts.append(jnp.broadcast_to(part, (128, 128)).T)
    return parts[0] if len(parts) == 1 else jnp.concatenate(parts, 0)


def one_hot(cols, first, width):
    rows = cols.shape[0]
    lane = lax.broadcasted_iota(jnp.int32, (rows, 128), 1).astype(F32)
    parts = []
    for start in range(first, first + width, 128):
        parts.append(jnp.where(cols == lane + float(start), 1.0, 0.0).astype(BF16))
    return parts[0] if len(parts) == 1 else jnp.concatenate(parts, 1)


def scatter_matrix(row):
    slots = lax.broadcasted_iota(jnp.int32, (M_DEV, row.shape[1]), 0)
    return jnp.where(slots == row, 1.0, 0.0).astype(BF16)


def node_update(rows, totals, first_own, first_sum, bias, second, gain):
    pre = dot(rows, first_own) + dot(totals.astype(BF16), first_sum) + bias
    hidden = silu(pre).astype(BF16)
    result = normalised(dot(hidden, second)) * gain
    return (rows.astype(F32) + result).astype(BF16)


def mesh_kernel(
    grid_nodes,
    mesh_nodes,
    grid_rim,
    mesh_rim,
    long_send,
    g2m_edges,
    short_edges,
    long_edges,
    edge_first,
    edge_second,
    edge_bias,
    edge_gain,
    node_first,
    node_second,
    node_bias,
    node_gain,
    dec_out,
    mesh_out,
    gq_out,
    gp_out,
    grid_v,
    mesh_v,
    grim_v,
    mrim_v,
    send_v,
    g2m_v,
    short_v,
    long_v,
    ef_v,
    es_v,
    eb_v,
    eg_v,
    nf_v,
    ns_v,
    nb_v,
    ng_v,
    enc_table,
    enc_halo,
    enc_rim,
    partial,
    cols_v,
    proj_v,
    short_table,
    short_rim,
    long_table,
    long_out,
    long_in,
    long_rows,
    dec_table,
    dec_rim,
    totals,
    gq_v,
    gp_v,
    in_sem,
    out_sem,
    halo_send,
    halo_recv,
    long_ssem,
    long_rsem,
):
    band = lax.axis_index("aa")
    sector = lax.axis_index("ba")
    me = band * N_BA + sector

    loads = {}

    def load(name, src, dst):
        copy = pltpu.make_async_copy(src, dst, in_sem.at[len(loads)])
        copy.start()
        loads[name] = copy

    load("grid", grid_nodes, grid_v)
    load("ef00", edge_first.at[0, 0], ef_v.at[0, 0])
    load("grim", grid_rim, grim_v)
    load("mesh", mesh_nodes, mesh_v)
    load("ef01", edge_first.at[0, 1], ef_v.at[0, 1])
    load("eb", edge_bias, eb_v)
    load("g2m", g2m_edges, g2m_v)
    load("mrim", mesh_rim, mrim_v)
    load("send", long_send, send_v)
    load("short", short_edges, short_v)
    load("long", long_edges, long_v)
    load("ef31", edge_first.at[3, 1], ef_v.at[3, 1])
    load("nf30", node_first.at[3, 0], nf_v.at[3, 0])
    load("nb", node_bias, nb_v)
    load("eg", edge_gain, eg_v)
    load("ng", node_gain, ng_v)
    load("es0", edge_second.at[0], es_v.at[0])
    load("nf0", node_first.at[0], nf_v.at[0])
    load("ns0", node_second.at[0], ns_v.at[0])
    load("ef1", edge_first.at[1], ef_v.at[1])
    load("es1", edge_second.at[1], es_v.at[1])
    load("nf1", node_first.at[1], nf_v.at[1])
    load("ns1", node_second.at[1], ns_v.at[1])
    load("ef2", edge_first.at[2], ef_v.at[2])
    load("es2", edge_second.at[2], es_v.at[2])
    load("nf2", node_first.at[2], nf_v.at[2])
    load("ns2", node_second.at[2], ns_v.at[2])
    load("ef30", edge_first.at[3, 0], ef_v.at[3, 0])

    barrier = pltpu.get_barrier_semaphore()

    def greet(step, carry):
        peer = lax.rem(me + step, DEVICES)
        pl.semaphore_signal(
            barrier, inc=1, device_id=(peer // N_BA, lax.rem(peer, N_BA)), device_id_type=MESH
        )
        return carry

    lax.fori_loop(1, DEVICES, greet, 0)

    def neighbour(k):
        return (
            lax.rem(band + (ALONG_FIRST[k] + N_AA), N_AA),
            lax.rem(sector + (ALONG_SECOND[k] + N_BA), N_BA),
        )

    def halo_copy(k, sem_base, rim, table, first, depth):
        return pltpu.make_async_remote_copy(
            src_ref=rim.at[pl.ds(k * depth, depth)],
            dst_ref=table.at[pl.ds(first + (7 - k) * depth, depth)],
            send_sem=halo_send.at[sem_base + k],
            recv_sem=halo_recv.at[sem_base + 7 - k],
            device_id=neighbour(k),
            device_id_type=MESH,
        )

    loads["grid"].wait()
    loads["ef00"].wait()
    for start in range(0, G_DEV, 512):
        enc_table[start : start + 512, :] = dot(grid_v[start : start + 512, :], ef_v[0, 0]).astype(BF16)
    loads["grim"].wait()
    copies = []
    for half in range(2):
        cols = jnp.concatenate([columns(grim_v[0, k : k + 1, :]) for k in range(4 * half, 4 * half + 4)], 0)
        enc_rim[half * 512 : half * 512 + 512, :] = dot(
            one_hot(cols, 0, G_DEV), enc_table[0:G_DEV, :]
        ).astype(BF16)
        if half == 0:
            pl.semaphore_wait(barrier, DEVICES - 1)
        for k in range(4 * half, 4 * half + 4):
            copy = halo_copy(k, 0, enc_rim, enc_halo, 0, GB)
            copy.start()
            copies.append(copy)

    loads["mesh"].wait()
    loads["ef01"].wait()
    loads["eb"].wait()
    enc_table[G_DEV : G_DEV + M_DEV, :] = (dot(mesh_v[...], ef_v[0, 1]) + eb_v[0:1, :]).astype(BF16)
    enc_table[G_DEV + M_DEV : G_DEV + 256, :] = jnp.zeros((64, D), BF16)
    proj_v[M_DEV:256, :] = jnp.zeros((64, D), BF16)
    loads["g2m"].wait()

    def enc_local(step, carry):
        start = pl.multiple_of(step * TILE, TILE)
        here = pl.ds(start, TILE)
        senders = columns(g2m_v[0, 0:1, here])
        cols_v[here, :] = senders
        targets = columns(g2m_v[0, 1:2, here])
        picks = jnp.concatenate([one_hot(senders, 0, G_DEV), one_hot(targets, 0, 256)], 1)
        partial[here, :] = dot(picks, enc_table[...])
        return carry

    lax.fori_loop(0, E_G2M // TILE, enc_local, 0)

    for name in ("ef31", "nf30", "nb"):
        loads[name].wait()
    for start in range(0, G_DEV, 512):
        rows = grid_v[start : start + 512, :]
        gq_v[start : start + 512, :] = (dot(rows, ef_v[3, 1]) + eb_v[3:4, :]).astype(BF16)
        gp_v[start : start + 512, :] = (dot(rows, nf_v[3, 0]) + nb_v[3:4, :]).astype(BF16)
    gq_copy = pltpu.make_async_copy(gq_v, gq_out, out_sem.at[0])
    gp_copy = pltpu.make_async_copy(gp_v, gp_out, out_sem.at[1])
    gq_copy.start()
    gp_copy.start()

    def add_messages(x, second, target_row):
        hidden = silu(x).astype(BF16)
        message = normalised(dot(hidden, second)).astype(BF16)
        totals[...] += dot(scatter_matrix(target_row), message)

    for name in ("eg", "ng", "es0", "nf0", "ns0"):
        loads[name].wait()
    totals[...] = jnp.zeros((M_DEV, D), F32)
    for copy in copies:
        copy.wait()

    def enc_remote(step, carry):
        start = pl.multiple_of(step * TILE, TILE)
        here = pl.ds(start, TILE)
        x = partial[here, :] + dot(one_hot(cols_v[here, :], G_DEV, 8 * GB), enc_halo[...])
        add_messages(x, es_v[0], g2m_v[0, 1:2, here])
        return carry

    lax.fori_loop(0, E_G2M // TILE, enc_remote, 0)

    def update(section):
        mesh_v[...] = node_update(
            mesh_v[...],
            totals[...] * eg_v[section : section + 1, :],
            nf_v[section, 0],
            nf_v[section, 1],
            nb_v[section : section + 1, :],
            ns_v[section],
            ng_v[section : section + 1, :],
        )

    update(0)

    loads["mrim"].wait()

    def rim_columns():
        parts = []
        sub = lax.broadcasted_iota(jnp.int32, (HB, HB), 0)
        lane = lax.broadcasted_iota(jnp.int32, (HB, HB), 1)
        for k in range(8):
            row = jnp.broadcast_to(mrim_v[0, k : k + 1, :].astype(F32), (HB, HB))
            col = jnp.sum(jnp.where(sub == lane, row, 0.0), axis=1, keepdims=True)
            parts.append(jnp.broadcast_to(col, (HB, 128)))
        return jnp.concatenate(parts, 0)

    def mesh_halo(section, sem_base, rim, table):
        proj = dot(mesh_v[...], ef_v[section, 0]).astype(BF16)
        proj_v[0:M_DEV, :] = proj
        table[0:M_DEV, :] = proj
        rim[...] = dot(one_hot(rim_columns(), 0, 128), proj_v[0:128, :]).astype(BF16)
        started = []
        for k in range(8):
            copy = halo_copy(k, sem_base, rim, table, M_DEV, HB)
            copy.start()
            started.append(copy)
        return started

    loads["ef1"].wait()
    copies = mesh_halo(1, 8, short_rim, short_table)
    short_table[M_DEV + 8 * HB : 512, :] = (dot(mesh_v[...], ef_v[1, 1]) + eb_v[1:2, :]).astype(BF16)
    for name in ("short", "es1", "nf1", "ns1"):
        loads[name].wait()
    totals[...] = jnp.zeros((M_DEV, D), F32)
    for copy in copies:
        copy.wait()

    def short_step(step, carry):
        start = pl.multiple_of(step * TILE, TILE)
        here = pl.ds(start, TILE)
        senders = columns(short_v[0, 0:1, here])
        targets = columns(short_v[0, 1:2, here]) + float(M_DEV + 8 * HB)
        lane = lax.broadcasted_iota(jnp.int32, (TILE, 128), 1).astype(F32)
        parts = []
        for first in range(0, 512, 128):
            place = lane + float(first)
            parts.append(
                jnp.where((senders == place) | (targets == place), 1.0, 0.0).astype(BF16)
            )
        x = dot(jnp.concatenate(parts, 1), short_table[...])
        add_messages(x, es_v[1], short_v[0, 1:2, here])
        return carry

    lax.fori_loop(0, E_MESH // TILE, short_step, 0)
    update(1)

    loads["ef2"].wait()
    loads["send"].wait()
    proj = dot(mesh_v[...], ef_v[2, 0]).astype(BF16)
    proj_v[0:M_DEV, :] = proj
    long_table[0:M_DEV, :] = proj
    lists = send_v[0].astype(F32).astype(BF16)
    for start in range(0, DEVICES * KL, 512):
        sub = lax.broadcasted_iota(jnp.int32, (512, DEVICES), 0) + start
        lane = lax.broadcasted_iota(jnp.int32, (512, DEVICES), 1)
        spread = dot(jnp.where(sub // KL == lane, 1.0, 0.0).astype(BF16), lists)
        sub = lax.broadcasted_iota(jnp.int32, (512, KL), 0)
        lane = lax.broadcasted_iota(jnp.int32, (512, KL), 1)
        col = jnp.sum(jnp.where(lax.rem(sub, KL) == lane, spread, 0.0), axis=1, keepdims=True)
        rows = dot(one_hot(jnp.broadcast_to(col, (512, 128)), 0, 128), proj_v[0:128, :])
        long_out[start // KL : (start + 512) // KL] = rows.reshape(512 // KL, KL, D).astype(BF16)

    def send_long(step, carry):
        peer = lax.rem(me + step, DEVICES)
        pltpu.make_async_remote_copy(
            src_ref=long_out.at[peer],
            dst_ref=long_in.at[me],
            send_sem=long_ssem,
            recv_sem=long_rsem,
            device_id=(peer // N_BA, lax.rem(peer, N_BA)),
            device_id_type=MESH,
        ).start()
        return carry

    lax.fori_loop(1, DEVICES, send_long, 0)
    long_in[me] = long_out[me]
    long_table[M_DEV : 2 * M_DEV, :] = (dot(mesh_v[...], ef_v[2, 1]) + eb_v[2:3, :]).astype(BF16)
    loads["long"].wait()

    def long_local(step, carry):
        start = pl.multiple_of(step * TILE, TILE)
        here = pl.ds(start, TILE)
        senders = columns(long_v[0, 0:1, here])
        cols_v[here, :] = senders
        own = jnp.where(senders < float(M_DEV), senders, -1.0)
        targets = columns(long_v[0, 1:2, here]) + float(M_DEV)
        lane = lax.broadcasted_iota(jnp.int32, (TILE, 128), 1).astype(F32)
        parts = []
        for first in range(0, 2 * M_DEV, 128):
            place = lane + float(first)
            parts.append(jnp.where((own == place) | (targets == place), 1.0, 0.0).astype(BF16))
        partial[here, :] = dot(jnp.concatenate(parts, 1), long_table[...])
        return carry

    lax.fori_loop(0, E_MESH // TILE, long_local, 0)
    for name in ("es2", "nf2", "ns2", "ef30"):
        loads[name].wait()
    totals[...] = jnp.zeros((M_DEV, D), F32)
    others = pl.ds(0, DEVICES - 1)
    pltpu.make_async_copy(long_out.at[others], long_out.at[others], long_ssem).wait()
    pltpu.make_async_copy(long_in.at[others], long_in.at[others], long_rsem).wait()
    for start in range(0, DEVICES, 32):
        block = long_in[start : start + 32].astype(F32).reshape(32 * KL, D)
        long_rows[start * KL : (start + 32) * KL, :] = block.astype(BF16)

    def long_remote(step, carry):
        start = pl.multiple_of(step * TILE, TILE)
        here = pl.ds(start, TILE)
        x = partial[here, :] + dot(one_hot(cols_v[here, :], M_DEV, DEVICES * KL), long_rows[...])
        add_messages(x, es_v[2], long_v[0, 1:2, here])
        return carry

    lax.fori_loop(0, E_MESH // TILE, long_remote, 0)
    update(2)

    copies = mesh_halo(3, 16, dec_rim, dec_table)
    dec_table[M_DEV + 8 * HB : 384, :] = jnp.zeros((64, D), BF16)
    mesh_copy = pltpu.make_async_copy(mesh_v, mesh_out, out_sem.at[2])
    mesh_copy.start()
    gq_copy.wait()
    gp_copy.wait()
    for copy in copies:
        copy.wait()
    dec_copy = pltpu.make_async_copy(dec_table, dec_out, out_sem.at[3])
    dec_copy.start()
    mesh_copy.wait()
    dec_copy.wait()


def mesh_part(
    grid_nodes,
    mesh_nodes,
    grid_rim,
    mesh_rim,
    long_send,
    g2m_edges,
    short_edges,
    long_edges,
    edge_first,
    edge_second,
    edge_bias,
    edge_gain,
    node_first,
    node_second,
    node_bias,
    node_gain,
):
    vmem = pltpu.VMEM
    anywhere = pl.BlockSpec(memory_space=pl.ANY)
    return pl.pallas_call(
        mesh_kernel,
        name="mesh_part",
        in_specs=[anywhere] * 16,
        out_specs=[anywhere] * 4,
        out_shape=[
            jax.ShapeDtypeStruct((384, D), BF16),
            jax.ShapeDtypeStruct((M_DEV, D), BF16),
            jax.ShapeDtypeStruct((G_DEV, D), BF16),
            jax.ShapeDtypeStruct((G_DEV, D), BF16),
        ],
        scratch_shapes=[
            vmem((G_DEV, D), BF16),
            vmem((M_DEV, D), BF16),
            vmem((1, 8, GB), jnp.int32),
            vmem((1, 8, HB), jnp.int32),
            vmem((1, DEVICES, KL), jnp.int32),
            vmem((1, 2, E_G2M), jnp.int32),
            vmem((1, 2, E_MESH), jnp.int32),
            vmem((1, 2, E_MESH), jnp.int32),
            vmem((4, 2, D, D), BF16),
            vmem((3, D, D), BF16),
            vmem((4, D), F32),
            vmem((4, D), F32),
            vmem((4, 2, D, D), BF16),
            vmem((3, D, D), BF16),
            vmem((4, D), F32),
            vmem((4, D), F32),
            vmem((G_DEV + 256, D), BF16),
            vmem((8 * GB, D), BF16),
            vmem((8 * GB, D), BF16),
            vmem((E_G2M, D), F32),
            vmem((E_G2M, 128), F32),
            vmem((256, D), BF16),
            vmem((512, D), BF16),
            vmem((8 * HB, D), BF16),
            vmem((2 * M_DEV, D), BF16),
            vmem((DEVICES, KL, D), BF16),
            vmem((DEVICES, KL, D), BF16),
            vmem((DEVICES * KL, D), BF16),
            vmem((384, D), BF16),
            vmem((8 * HB, D), BF16),
            vmem((M_DEV, D), F32),
            vmem((G_DEV, D), BF16),
            vmem((G_DEV, D), BF16),
            pltpu.SemaphoreType.DMA((28,)),
            pltpu.SemaphoreType.DMA((4,)),
            pltpu.SemaphoreType.DMA((24,)),
            pltpu.SemaphoreType.DMA((24,)),
            pltpu.SemaphoreType.DMA,
            pltpu.SemaphoreType.DMA,
        ],
        compiler_params=pltpu.CompilerParams(
            collective_id=0, has_side_effects=True, vmem_limit_bytes=60 * 1024 * 1024
        ),
    )(
        grid_nodes,
        mesh_nodes,
        grid_rim,
        mesh_rim,
        long_send,
        g2m_edges,
        short_edges,
        long_edges,
        edge_first,
        edge_second,
        edge_bias,
        edge_gain,
        node_first,
        node_second,
        node_bias,
        node_gain,
    )


DEC_TILE = 256


def decode_kernel(
    owned,
    edges,
    table,
    gq,
    gp,
    grid_rows,
    mesh_rows,
    edge_second,
    node_sum,
    node_second,
    edge_gain,
    node_gain,
    grid_out,
    mesh_out,
):
    step = pl.program_id(0)

    @pl.when(step == 0)
    def _():
        slot = lax.broadcasted_iota(jnp.int32, (M_DEV, D), 0)
        mesh_out[...] = jnp.where(slot < owned[0], mesh_rows[...].astype(F32), 0.0).astype(BF16)

    start = pl.multiple_of(step * DEC_TILE, DEC_TILE)
    total = jnp.zeros((DEC_TILE, D), F32)
    target = gq[...].astype(F32)
    for k in range(3):
        cols = columns(edges[0, k : k + 1, pl.ds(start, DEC_TILE)])
        x = dot(one_hot(cols, 0, 384), table[...]) + target
        hidden = silu(x).astype(BF16)
        total = total + normalised(dot(hidden, edge_second[0]))
    total = total * edge_gain[3:4, :]
    pre = gp[...].astype(F32) + dot(total.astype(BF16), node_sum[0, 0])
    hidden = silu(pre).astype(BF16)
    result = normalised(dot(hidden, node_second[0])) * node_gain[3:4, :]
    grid_out[...] = (grid_rows[...].astype(F32) + result).astype(BF16)


def decode_part(owned, edges, table, gq, gp, grid_rows, mesh_rows, es, nf, ns, eg, ng):
    def whole(*shape):
        return pl.BlockSpec(shape, lambda i: (0,) * len(shape))

    def tiled():
        return pl.BlockSpec((DEC_TILE, D), lambda i: (i, 0))

    return pl.pallas_call(
        decode_kernel,
        name="decode_part",
        grid=(G_DEV // DEC_TILE,),
        in_specs=[
            pl.BlockSpec(memory_space=pltpu.SMEM),
            whole(1, 3, G_DEV),
            whole(384, D),
            tiled(),
            tiled(),
            tiled(),
            whole(M_DEV, D),
            pl.BlockSpec((1, D, D), lambda i: (3, 0, 0)),
            pl.BlockSpec((1, 1, D, D), lambda i: (3, 1, 0, 0)),
            pl.BlockSpec((1, D, D), lambda i: (3, 0, 0)),
            whole(4, D),
            whole(4, D),
        ],
        out_specs=[tiled(), whole(M_DEV, D)],
        out_shape=[
            jax.ShapeDtypeStruct((G_DEV, D), BF16),
            jax.ShapeDtypeStruct((M_DEV, D), BF16),
        ],
    )(owned, edges, table, gq, gp, grid_rows, mesh_rows, es, nf, ns, eg, ng)


def per_device(
    grid_nodes,
    mesh_nodes,
    owned_nodes,
    grid_rim,
    mesh_rim,
    long_send,
    g2m_edges,
    short_edges,
    long_edges,
    m2g_edges,
    edge_first,
    edge_second,
    edge_bias,
    edge_gain,
    node_first,
    node_second,
    node_bias,
    node_gain,
):
    table, mesh_three, gq, gp = mesh_part(
        grid_nodes,
        mesh_nodes,
        grid_rim,
        mesh_rim,
        long_send,
        g2m_edges,
        short_edges,
        long_edges,
        edge_first,
        edge_second,
        edge_bias,
        edge_gain,
        node_first,
        node_second,
        node_bias,
        node_gain,
    )
    grid_out, mesh_out = decode_part(
        owned_nodes,
        m2g_edges,
        table,
        gq,
        gp,
        grid_nodes,
        mesh_three,
        edge_second,
        node_first,
        node_second,
        edge_gain,
        node_gain,
    )
    return (grid_out, mesh_out)


def solution(mesh):
    rows = P(("aa", "ba"), None)
    lists = P(("aa", "ba"), None, None)
    in_specs = (rows, rows, P(("aa", "ba"))) + (lists,) * 7 + (P(),) * 8
    return jax.shard_map(
        per_device, mesh=mesh, in_specs=in_specs, out_specs=(rows, rows), check_vma=False
    )
```

time: 248 us -> 87.7 us (0.35)
  matrix products: 104 us -> 0 us
  Pallas kernels: 0 us -> 83.4 us
  other arithmetic: 41 us -> 0 us
  local copies, waits for them, and re-layouts: 43 us -> 2.72 us
  starting transfers between devices: 35.3 us -> 0 us
  waiting for transfers between devices: 20 us -> 0 us
    dot_general x59 -> x0, matrix products: 104 us -> none  [the longest x24 40.2 us: one_block(): jnp.dot(member.astype(table.dtype), table, preferred_element_type=jnp.flo...]
    pallas_call x0 -> x2, Pallas kernels: none -> 83.4 us  [the longest x1 71.6 us: mesh_part(): pl.pallas_call(mesh_kernel, name='mesh_part', in_specs=[anywhere] * 16, o...]
    ppermute x12 -> x0, starting transfers between devices: 26.3 us -> none  [the longest x6 22.9 us: extended_2(): after = lax.ppermute(initial, axis, down)]
    convert_element_type x8 -> x0, other arithmetic: 16.3 us -> none  [the longest x4 12.2 us: messages(): jax.nn.silu(gathered.astype(jnp.float32) + target_proj + biases)]
    all_to_all x1 -> x0, waiting for transfers between devices: 14.1 us -> none  [per_device(): lax.all_to_all(outgoing, ('aa', 'ba'), split_axis=0, concat_axis=0, tiled...]
    unnamed x98 -> x2, local copies, waits for them, and re-layouts: 15.8 us -> 2.72 us
    dynamic_slice x34 -> x0, local copies, waits for them, and re-layouts: 10.8 us -> none  [pick_rows(): picked = lax.map(one_block, blocked_ids)]
    concatenate x8 -> x0, other arithmetic: 9.94 us -> none  [the longest x1 3.54 us: per_device(): repeated = jnp.concatenate([grid_target, grid_target, grid_target], 0)]
  transfers between devices with their start and end apart: 13 -> 0, of which waited for: 4 -> 0; matrix products, arithmetic and copies ran while one was open for 18% -> 0% of each run, Pallas kernels for 0% -> 0%
where the time goes in v1:
time: 87.7 us; the launch traced here: 87.5 us
  Pallas kernels  83.4 us (95%)
  local copies, waits for them, and re-layouts  2.72 us (3%)
  between operations  1.29 us (1%)
    pallas_call x1, Pallas kernels, mesh_part(): pl.pallas_call(mesh_kernel, name='mesh_part', in_specs=[anywhere] * 16, o...  71.6 us
    pallas_call x1, Pallas kernels, decode_part(): pl.pallas_call(decode_kernel, name='decode_part', grid=(G_DEV // DEC_TILE...  11.9 us
    unnamed x2, local copies, waits for them, and re-layouts  2.72 us

profile of v1, /device:TPU:0, one launch (start us, length us, event | category | flops | bytes accessed | tf_op | source)
XLA Modules:
  0.0 87.5 jit_solution(1255336316568707637)
XLA Ops:
  1.3 1.3 %copy.21.edges = s32[1,3,1024]{2,1,0:T(4,128)} copy(s32[1,3,1024]{2,0,1:T(1,128)} %param.27) | data formatting | bytes 24576 | tf_op args[9]
  2.6 1.4 %copy.20.long_send = s32[1,128,8]{2,1,0:T(8,128)} copy(s32[1,128,8]{1,2,0:T(8,128)} %param.23) | data formatting | bytes 8192 | tf_op args[5]
  4.0 71.6 %mesh_part.1 = (bf16[384,512]{1,0:T(8,128)(2,1)}, bf16[192,512]{1,0:T(8,128)(2,1)}, bf16[1024,512]{1,0:T(8,128)(2,1)}, bf16[1024,512]{1,0:T(8,128)(2,1)}) custom-call(bf16[1024,512]{1,0:T(8,128)(2,1)} %grid_rows.1, bf16[192,512]{1,0:T(8,128)(2,1)} %mesh_nodes.1, s32[1,8,128]{2,1,0:T(8,128)} %grid_rim.1, s32[1,8,16]{2,1,0:T(8,128)} %mesh_rim.1, ...), custom_call_target="tpu_custom_call" | custom-call | tf_op jit(solution)/shard_map/mesh_part/pallas_call | solution.py:439
  75.6 11.9 %decode_part.1 = (bf16[1024,512]{1,0:T(8,128)(2,1)}, bf16[192,512]{1,0:T(8,128)(2,1)}) custom-call(s32[1]{0:T(128)S(6)} %copy.22.owned, s32[1,3,1024]{2,1,0:T(4,128)} %copy.21.edges, bf16[384,512]{1,0:T(8,128)(2,1)} %get-tuple-element.6.table, bf16[1024,512]{1,0:T(8,128)(2,1)} %get-tuple-element.7.gq, bf16[1024,512]{1,0:T(8,128)(2,1)} %get-tuple-element.8.gp, ...), custom_call_target="tpu_custom_call" | custom-call | tf_op jit(solution)/shard_map/decode_part/pallas_call | solution.py:562

commit v2 on v1

v2 whole, which is shorter than its diff:
```python
import jax
import jax.numpy as jnp
from jax import lax
from jax.experimental import pallas as pl
from jax.experimental.pallas import tpu as pltpu
from jax.sharding import PartitionSpec as P

EPSILON = 1e-05
D = 512
G_DEV = 1024
M_DEV = 192
GB = 128
HB = 16
KL = 8
CS = 16
N_AA = 8
N_BA = 16
DEVICES = 128
E_G2M = 3072
E_MESH = 1536
TILE = 512
ALONG_FIRST = (-1, -1, -1, 0, 0, 1, 1, 1)
ALONG_SECOND = (-1, 0, 1, -1, 1, -1, 0, 1)
F32 = jnp.float32
BF16 = jnp.bfloat16
MESH = pl.DeviceIdType.MESH


def hops(first, second):
    steps = ((first + 1) // 2, second // 4, second % 4)
    return sum(min(step, 4 - step) for step in steps)


PEERS = sorted(
    [(a, b) for a in range(N_AA) for b in range(N_BA) if (a, b) != (0, 0)],
    key=lambda peer: -hops(*peer),
)


def dot(a, b):
    return jnp.dot(a, b, preferred_element_type=F32)


def silu(x):
    half = (0.5 * x).astype(BF16)
    return half * jnp.tanh(half) + half


def centred_weights(weights):
    wide = weights.astype(F32)
    return (wide - jnp.mean(wide, axis=-1, keepdims=True)).astype(BF16)


def normalised(centred):
    spread = jnp.mean(centred * centred, axis=-1, keepdims=True)
    return centred * lax.rsqrt(spread + EPSILON)


def columns(row):
    parts = []
    for start in range(0, row.shape[1], 128):
        part = row[:, start : start + 128].astype(F32)
        parts.append(jnp.broadcast_to(part, (128, 128)).T)
    return parts[0] if len(parts) == 1 else jnp.concatenate(parts, 0)


def split_ids(cols):
    block = jnp.floor(cols * (1.0 / 256.0))
    return block.astype(BF16), (cols - 256.0 * block).astype(BF16)


def one_hot(cols, first, width):
    rows = cols.shape[0]
    block, place = split_ids(cols)
    lane = lax.broadcasted_iota(jnp.int32, (rows, 128), 1).astype(F32)
    lanes = (lane.astype(BF16), (lane + 128.0).astype(BF16))
    one, zero = jnp.ones((), BF16), jnp.zeros((), BF16)
    parts = []
    for start in range(first, first + width, 256):
        here = jnp.where(block == jnp.asarray(start // 256, BF16), place, jnp.asarray(-1, BF16))
        for half in range(2):
            if start + 128 * half < first + width:
                parts.append(jnp.where(here == lanes[half], one, zero))
    return parts[0] if len(parts) == 1 else jnp.concatenate(parts, 1)


def scatter_matrix(row):
    slots = lax.broadcasted_iota(jnp.int32, (M_DEV, row.shape[1]), 0)
    return jnp.where(slots == row, 1.0, 0.0).astype(BF16)


def node_update(rows, totals, first_own, first_sum, bias, second, gain):
    pre = dot(rows, first_own) + dot(totals.astype(BF16), first_sum) + bias
    hidden = silu(pre)
    result = normalised(dot(hidden, second)) * gain
    return (rows.astype(F32) + result).astype(BF16)


def mesh_kernel(
    grid_nodes,
    mesh_nodes,
    grid_rim,
    mesh_rim,
    long_send,
    g2m_edges,
    short_edges,
    long_edges,
    m2g_edges,
    edge_first,
    edge_second,
    edge_bias,
    edge_gain,
    node_first,
    node_second,
    node_bias,
    node_gain,
    dec_out,
    mesh_out,
    gq_out,
    gp_out,
    picks_out,
    second_out,
    grid_v,
    mesh_v,
    grim_v,
    mrim_v,
    send_v,
    g2m_v,
    short_v,
    long_v,
    m2g_v,
    ef_v,
    es_v,
    eb_v,
    eg_v,
    nf_v,
    ns_v,
    nb_v,
    ng_v,
    enc_table,
    enc_halo,
    enc_rim,
    partial,
    picks_v,
    hidden_v,
    proj_v,
    coarse_v,
    rim_picks,
    short_table,
    short_rim,
    long_table,
    long_out,
    long_in,
    long_rows,
    dec_table,
    dec_rim,
    dec_picks,
    totals,
    gq_v,
    gp_v,
    in_sem,
    out_sem,
    halo_send,
    halo_recv,
    long_ssem,
    long_rsem,
    spread_sem,
):
    band = lax.axis_index("aa")
    sector = lax.axis_index("ba")
    me = band * N_BA + sector

    loads = {}

    def load(name, src, dst):
        copy = pltpu.make_async_copy(src, dst, in_sem.at[len(loads)])
        copy.start()
        loads[name] = copy

    def arrived(*names):
        for name in names:
            loads[name].wait()

    def at(first, second):
        return (
            lax.rem(band + (first + N_AA), N_AA),
            lax.rem(sector + (second + N_BA), N_BA),
        )

    def greet(semaphore, stride_first, stride_second, around):
        for k in around:
            pl.semaphore_signal(
                semaphore,
                inc=1,
                device_id=at(stride_first * ALONG_FIRST[k], stride_second * ALONG_SECOND[k]),
                device_id_type=MESH,
            )

    barrier = pltpu.get_barrier_semaphore()
    greet(barrier, 1, 1, range(8))

    load("grim", grid_rim, grim_v)
    load("grid", grid_nodes, grid_v)
    load("ef00", edge_first.at[0, 0], ef_v.at[0, 0])
    load("mesh", mesh_nodes, mesh_v)
    load("ef01", edge_first.at[0, 1], ef_v.at[0, 1])
    load("eb", edge_bias, eb_v)
    load("g2m", g2m_edges, g2m_v)
    load("es0", edge_second.at[0], es_v.at[0])
    load("ns0", node_second.at[0], ns_v.at[0])
    load("nf0", node_first.at[0], nf_v.at[0])
    load("eg", edge_gain, eg_v)
    load("ng", node_gain, ng_v)
    load("nb", node_bias, nb_v)
    load("mrim", mesh_rim, mrim_v)
    load("ef1", edge_first.at[1], ef_v.at[1])
    load("short", short_edges, short_v)
    load("es1", edge_second.at[1], es_v.at[1])
    load("nf1", node_first.at[1], nf_v.at[1])
    load("ns1", node_second.at[1], ns_v.at[1])
    load("send", long_send, send_v)
    load("ef2", edge_first.at[2], ef_v.at[2])
    load("long", long_edges, long_v)
    load("es2", edge_second.at[2], es_v.at[2])
    load("nf2", node_first.at[2], nf_v.at[2])
    load("ns2", node_second.at[2], ns_v.at[2])
    load("ef3", edge_first.at[3], ef_v.at[3])
    load("nf30", node_first.at[3, 0], nf_v.at[3, 0])
    load("es3", edge_second.at[3], es_v.at[3])
    load("ns3", node_second.at[3], ns_v.at[3])
    load("m2g", m2g_edges, m2g_v)

    def halo_copy(k, sem_base, rim, table, first, depth):
        return pltpu.make_async_remote_copy(
            src_ref=rim.at[pl.ds(k * depth, depth)],
            dst_ref=table.at[pl.ds(first + (7 - k) * depth, depth)],
            send_sem=halo_send.at[sem_base + k],
            recv_sem=halo_recv.at[sem_base + 7 - k],
            device_id=at(ALONG_FIRST[k], ALONG_SECOND[k]),
            device_id_type=MESH,
        )

    copies = []
    arrived("grim", "grid")
    for pair in ((3, 4), (0, 7), (2, 5), (1, 6)):
        cols = jnp.concatenate([columns(grim_v[0, k : k + 1, :]) for k in pair], 0)
        rows = dot(one_hot(cols, 0, G_DEV), grid_v[...]).astype(BF16)
        if not copies:
            arrived("ef00")
        rows = dot(rows, ef_v[0, 0]).astype(BF16)
        for place, k in enumerate(pair):
            enc_rim[k * GB : (k + 1) * GB, :] = rows[place * GB : (place + 1) * GB, :]
        if not copies:
            pl.semaphore_wait(barrier, 8)
        for k in pair:
            copy = halo_copy(k, 0, enc_rim, enc_halo, 0, GB)
            copy.start()
            copies.append(copy)
    greet(spread_sem.at[0], 1, 1, range(8))

    for start in range(0, G_DEV, 512):
        enc_table[start : start + 512, :] = dot(grid_v[start : start + 512, :], ef_v[0, 0]).astype(BF16)
    arrived("mesh", "ef01", "eb")
    enc_table[G_DEV : G_DEV + M_DEV, :] = (dot(mesh_v[...], ef_v[0, 1]) + eb_v[0:1, :]).astype(BF16)
    enc_table[G_DEV + M_DEV : G_DEV + 256, :] = jnp.zeros((64, D), BF16)
    proj_v[M_DEV:256, :] = jnp.zeros((64, D), BF16)
    coarse_v[...] = jnp.zeros((128, D), BF16)
    arrived("g2m")

    def enc_local(step, carry):
        start = pl.multiple_of(step * TILE, TILE)
        here = pl.ds(start, TILE)
        senders = columns(g2m_v[0, 0:1, here])
        targets = columns(g2m_v[0, 1:2, here])
        picks = jnp.concatenate([one_hot(senders, 0, G_DEV), one_hot(targets, 0, 256)], 1)
        partial[here, :] = dot(picks, enc_table[...])
        picks_v[here, :] = one_hot(senders, G_DEV, 8 * GB)
        return carry

    lax.fori_loop(0, E_G2M // TILE, enc_local, 0)

    def centre(section):
        es_v[section] = centred_weights(es_v[section])
        ns_v[section] = centred_weights(ns_v[section])

    arrived("es0", "ns0")
    centre(0)
    arrived("mrim")
    sub = lax.broadcasted_iota(jnp.int32, (HB, HB), 0)
    lane = lax.broadcasted_iota(jnp.int32, (HB, HB), 1)
    parts = []
    for k in range(8):
        row = jnp.broadcast_to(mrim_v[0, k : k + 1, :].astype(F32), (HB, HB))
        col = jnp.sum(jnp.where(sub == lane, row, 0.0), axis=1, keepdims=True)
        parts.append(jnp.broadcast_to(col, (HB, 128)))
    rim_picks[...] = one_hot(jnp.concatenate(parts, 0), 0, 128)
    arrived("es1", "ns1")
    centre(1)

    def produce(x):
        hidden_v[...] = silu(x)

    def consume(section, edges, start):
        message = normalised(dot(hidden_v[...], es_v[section])).astype(BF16)
        totals[...] += dot(scatter_matrix(edges[0, 1:2, pl.ds(start, TILE)]), message)

    def rounds(section, edges, count, picked):
        totals[...] = jnp.zeros((M_DEV, D), F32)
        produce(picked(0))

        def step(index, carry):
            start = pl.multiple_of(index * TILE, TILE)
            consume(section, edges, pl.multiple_of(start - TILE, TILE))
            produce(picked(start))
            return carry

        lax.fori_loop(1, count, step, 0)
        consume(section, edges, (count - 1) * TILE)

    def updated(section, rows, sums):
        return node_update(
            rows,
            sums * eg_v[section : section + 1, :],
            nf_v[section, 0],
            nf_v[section, 1],
            nb_v[section : section + 1, :],
            ns_v[section],
            ng_v[section : section + 1, :],
        )

    arrived("nf0", "eg", "ng", "nb")
    pl.semaphore_wait(spread_sem.at[0], 8)
    greet(spread_sem.at[1], 2, 2, range(8))
    for copy in copies:
        copy.wait()

    def enc_picked(start):
        here = pl.ds(start, TILE)
        return partial[here, :] + dot(picks_v[here, :], enc_halo[...])

    rounds(0, g2m_v, E_G2M // TILE, enc_picked)
    mesh_v[...] = updated(0, mesh_v[...], totals[...])

    def mesh_halo(section, sem_base, rim, table):
        proj = dot(mesh_v[...], ef_v[section, 0]).astype(BF16)
        proj_v[0:M_DEV, :] = proj
        rim[...] = dot(rim_picks[...], proj_v[0:128, :]).astype(BF16)
        started = []
        for k in range(8):
            copy = halo_copy(k, sem_base, rim, table, M_DEV, HB)
            copy.start()
            started.append(copy)
        table[0:M_DEV, :] = proj
        return started

    arrived("ef1")
    copies = mesh_halo(1, 8, short_rim, short_table)
    short_table[M_DEV + 8 * HB : 512, :] = (dot(mesh_v[...], ef_v[1, 1]) + eb_v[1:2, :]).astype(BF16)
    arrived("short")

    def double_one_hot(first, second, width):
        rows = first.shape[0]
        one_block, one_place = split_ids(first)
        two_block, two_place = split_ids(second)
        lane = lax.broadcasted_iota(jnp.int32, (rows, 128), 1).astype(F32)
        lanes = (lane.astype(BF16), (lane + 128.0).astype(BF16))
        one, zero, none = jnp.ones((), BF16), jnp.zeros((), BF16), jnp.asarray(-1, BF16)
        parts = []
        for start in range(0, width, 128):
            group = jnp.asarray(start // 256, BF16)
            here = lanes[start // 128 % 2]
            one_here = jnp.where(one_block == group, one_place, none)
            two_here = jnp.where(two_block == group, two_place, none)
            parts.append(jnp.where((one_here == here) | (two_here == here), one, zero))
        return jnp.concatenate(parts, 1)

    def short_picks(step, carry):
        here = pl.ds(pl.multiple_of(step * TILE, TILE), TILE)
        senders = columns(short_v[0, 0:1, here])
        targets = columns(short_v[0, 1:2, here]) + float(M_DEV + 8 * HB)
        picks_v[here, 0:512] = double_one_hot(senders, targets, 512)
        return carry

    lax.fori_loop(0, E_MESH // TILE, short_picks, 0)
    arrived("es2", "ns2", "nf1")
    centre(2)
    pl.semaphore_wait(spread_sem.at[1], 8)
    greet(spread_sem.at[2], 0, 4, (3, 4))
    for copy in copies:
        copy.wait()

    def short_picked(start):
        return dot(picks_v[pl.ds(start, TILE), 0:512], short_table[...])

    rounds(1, short_v, E_MESH // TILE, short_picked)

    arrived("ef2", "send")
    coarse = updated(1, mesh_v[0:CS, :], totals[0:CS, :])
    coarse_v[0:CS, :] = dot(coarse, ef_v[2, 0]).astype(BF16)
    lists = send_v[0].astype(F32).astype(BF16)
    for start in range(0, DEVICES * KL, 512):
        sub = lax.broadcasted_iota(jnp.int32, (512, DEVICES), 0) + start
        lane = lax.broadcasted_iota(jnp.int32, (512, DEVICES), 1)
        owner = jnp.where(sub // KL == lane, 1.0, 0.0).astype(BF16)
        listed = lax.dot_general(owner, lists, (((1,), (1,)), ((), ())), preferred_element_type=F32)
        sub = lax.broadcasted_iota(jnp.int32, (512, KL), 0)
        lane = lax.broadcasted_iota(jnp.int32, (512, KL), 1)
        col = jnp.sum(jnp.where(lax.rem(sub, KL) == lane, listed, 0.0), axis=1, keepdims=True)
        rows = dot(one_hot(jnp.broadcast_to(col, (512, 128)), 0, 128), coarse_v[...])
        long_out[start // KL : (start + 512) // KL] = rows.reshape(512 // KL, KL, D).astype(BF16)
    pl.semaphore_wait(spread_sem.at[2], 2)
    for first, second in PEERS:
        peer_first = lax.rem(band + first, N_AA)
        peer_second = (sector // 4 + second // 4) % 4 * 4 + (sector + second) % 4
        pltpu.make_async_remote_copy(
            src_ref=long_out.at[peer_first * N_BA + peer_second],
            dst_ref=long_in.at[me],
            send_sem=long_ssem,
            recv_sem=long_rsem,
            device_id=(peer_first, peer_second),
            device_id_type=MESH,
        ).start()
    long_in[me] = long_out[me]

    mesh_v[...] = updated(1, mesh_v[...], totals[...])
    long_table[0:M_DEV, :] = dot(mesh_v[...], ef_v[2, 0]).astype(BF16)
    long_table[M_DEV : 2 * M_DEV, :] = (dot(mesh_v[...], ef_v[2, 1]) + eb_v[2:3, :]).astype(BF16)
    arrived("long")

    def long_local(step, carry):
        here = pl.ds(pl.multiple_of(step * TILE, TILE), TILE)
        senders = columns(long_v[0, 0:1, here])
        own = jnp.where(senders < float(M_DEV), senders, -1.0)
        targets = columns(long_v[0, 1:2, here]) + float(M_DEV)
        partial[here, :] = dot(double_one_hot(own, targets, 2 * M_DEV), long_table[...])
        away = jnp.where(senders < float(M_DEV), -1.0, senders - float(M_DEV))
        picks_v[here, :] = one_hot(away, 0, DEVICES * KL)
        return carry

    lax.fori_loop(0, E_MESH // TILE, long_local, 0)
    arrived("ef3", "nf30", "es3", "ns3", "m2g")
    for start in range(0, G_DEV, 512):
        rows = grid_v[start : start + 512, :]
        gq_v[start : start + 512, :] = (dot(rows, ef_v[3, 1]) + eb_v[3:4, :]).astype(BF16)
        gp_v[start : start + 512, :] = (dot(rows, nf_v[3, 0]) + nb_v[3:4, :]).astype(BF16)
    centre(3)
    gq_copy = pltpu.make_async_copy(gq_v, gq_out, out_sem.at[0])
    gp_copy = pltpu.make_async_copy(gp_v, gp_out, out_sem.at[1])
    es_copy = pltpu.make_async_copy(es_v.at[3], second_out.at[0], out_sem.at[2])
    ns_copy = pltpu.make_async_copy(ns_v.at[3], second_out.at[1], out_sem.at[3])
    outs = [gq_copy, gp_copy, es_copy, ns_copy]

    def dec_ids(step, carry):
        here = pl.ds(pl.multiple_of(step * 512, 512), 512)
        for k in range(3):
            dec_picks[k, here, :] = one_hot(columns(m2g_v[k, :, here]), 0, 384)
        return carry

    lax.fori_loop(0, G_DEV // 512, dec_ids, 0)
    outs.append(pltpu.make_async_copy(dec_picks, picks_out, out_sem.at[4]))
    for copy in outs:
        copy.start()
    arrived("nf2")
    others = pl.ds(0, DEVICES - 1)
    pltpu.make_async_copy(long_out.at[others], long_out.at[others], long_ssem).wait()
    pltpu.make_async_copy(long_in.at[others], long_in.at[others], long_rsem).wait()
    for start in range(0, DEVICES, 32):
        block = long_in[start : start + 32].astype(F32).reshape(32 * KL, D)
        long_rows[start * KL : (start + 32) * KL, :] = block.astype(BF16)

    def long_picked(start):
        here = pl.ds(start, TILE)
        return partial[here, :] + dot(picks_v[here, :], long_rows[...])

    rounds(2, long_v, E_MESH // TILE, long_picked)
    mesh_v[...] = updated(2, mesh_v[...], totals[...])

    copies = mesh_halo(3, 16, dec_rim, dec_table)
    dec_table[M_DEV + 8 * HB : 384, :] = jnp.zeros((64, D), BF16)
    outs.append(pltpu.make_async_copy(mesh_v, mesh_out, out_sem.at[5]))
    outs[-1].start()
    for copy in outs:
        copy.wait()
    for copy in copies:
        copy.wait()
    dec_copy = pltpu.make_async_copy(dec_table, dec_out, out_sem.at[6])
    dec_copy.start()
    dec_copy.wait()


def mesh_part(*operands):
    vmem = pltpu.VMEM
    anywhere = pl.BlockSpec(memory_space=pl.ANY)
    return pl.pallas_call(
        mesh_kernel,
        name="mesh_part",
        in_specs=[anywhere] * 17,
        out_specs=[anywhere] * 6,
        out_shape=[
            jax.ShapeDtypeStruct((384, D), BF16),
            jax.ShapeDtypeStruct((M_DEV, D), BF16),
            jax.ShapeDtypeStruct((G_DEV, D), BF16),
            jax.ShapeDtypeStruct((G_DEV, D), BF16),
            jax.ShapeDtypeStruct((3, G_DEV, 384), BF16),
            jax.ShapeDtypeStruct((2, D, D), BF16),
        ],
        scratch_shapes=[
            vmem((G_DEV, D), BF16),
            vmem((M_DEV, D), BF16),
            vmem((1, 8, GB), jnp.int32),
            vmem((1, 8, HB), jnp.int32),
            vmem((1, KL, DEVICES), jnp.int32),
            vmem((1, 2, E_G2M), jnp.int32),
            vmem((1, 2, E_MESH), jnp.int32),
            vmem((1, 2, E_MESH), jnp.int32),
            vmem((3, 1, G_DEV), jnp.int32),
            vmem((4, 2, D, D), BF16),
            vmem((4, D, D), BF16),
            vmem((4, D), F32),
            vmem((4, D), F32),
            vmem((4, 2, D, D), BF16),
            vmem((4, D, D), BF16),
            vmem((4, D), F32),
            vmem((4, D), F32),
            vmem((G_DEV + 256, D), BF16),
            vmem((8 * GB, D), BF16),
            vmem((8 * GB, D), BF16),
            vmem((E_G2M, D), F32),
            vmem((E_G2M, 8 * GB), BF16),
            vmem((TILE, D), BF16),
            vmem((256, D), BF16),
            vmem((128, D), BF16),
            vmem((128, 128), BF16),
            vmem((512, D), BF16),
            vmem((8 * HB, D), BF16),
            vmem((2 * M_DEV, D), BF16),
            vmem((DEVICES, KL, D), BF16),
            vmem((DEVICES, KL, D), BF16),
            vmem((DEVICES * KL, D), BF16),
            vmem((384, D), BF16),
            vmem((8 * HB, D), BF16),
            vmem((3, G_DEV, 384), BF16),
            vmem((M_DEV, D), F32),
            vmem((G_DEV, D), BF16),
            vmem((G_DEV, D), BF16),
            pltpu.SemaphoreType.DMA((30,)),
            pltpu.SemaphoreType.DMA((7,)),
            pltpu.SemaphoreType.DMA((24,)),
            pltpu.SemaphoreType.DMA((24,)),
            pltpu.SemaphoreType.DMA,
            pltpu.SemaphoreType.DMA,
            pltpu.SemaphoreType.REGULAR((3,)),
        ],
        compiler_params=pltpu.CompilerParams(
            collective_id=0, has_side_effects=True, vmem_limit_bytes=60 * 1024 * 1024
        ),
    )(*operands)


DEC_TILE = 256


def decode_kernel(
    owned,
    picks,
    table,
    gq,
    gp,
    grid_rows,
    mesh_rows,
    seconds,
    node_sum,
    edge_gain,
    node_gain,
    grid_out,
    mesh_out,
):
    @pl.when(pl.program_id(0) == 0)
    def _():
        slot = lax.broadcasted_iota(jnp.int32, (M_DEV, D), 0)
        mesh_out[...] = jnp.where(slot < owned[0], mesh_rows[...].astype(F32), 0.0).astype(BF16)

    target = gq[...].astype(F32)
    x = dot(picks[...].reshape(3 * DEC_TILE, 384), table[...])
    hidden = silu(x + jnp.concatenate([target] * 3, 0))
    message = normalised(dot(hidden, seconds[0]))
    total = message[0:DEC_TILE] + message[DEC_TILE : 2 * DEC_TILE] + message[2 * DEC_TILE :]
    total = total * edge_gain[3:4, :]
    pre = gp[...].astype(F32) + dot(total.astype(BF16), node_sum[0, 0])
    result = normalised(dot(silu(pre), seconds[1])) * node_gain[3:4, :]
    grid_out[...] = (grid_rows[...].astype(F32) + result).astype(BF16)


def decode_part(owned, picks, table, gq, gp, grid_rows, mesh_rows, seconds, nf, eg, ng):
    def whole(*shape):
        return pl.BlockSpec(shape, lambda i: (0,) * len(shape))

    def tiled():
        return pl.BlockSpec((DEC_TILE, D), lambda i: (i, 0))

    return pl.pallas_call(
        decode_kernel,
        name="decode_part",
        grid=(G_DEV // DEC_TILE,),
        in_specs=[
            pl.BlockSpec(memory_space=pltpu.SMEM),
            pl.BlockSpec((3, DEC_TILE, 384), lambda i: (0, i, 0)),
            whole(384, D),
            tiled(),
            tiled(),
            tiled(),
            whole(M_DEV, D),
            whole(2, D, D),
            pl.BlockSpec((1, 1, D, D), lambda i: (3, 1, 0, 0)),
            whole(4, D),
            whole(4, D),
        ],
        out_specs=[tiled(), whole(M_DEV, D)],
        out_shape=[
            jax.ShapeDtypeStruct((G_DEV, D), BF16),
            jax.ShapeDtypeStruct((M_DEV, D), BF16),
        ],
    )(owned, picks, table, gq, gp, grid_rows, mesh_rows, seconds, nf, eg, ng)


def per_device(
    grid_nodes,
    mesh_nodes,
    owned_nodes,
    grid_rim,
    mesh_rim,
    long_send,
    g2m_edges,
    short_edges,
    long_edges,
    m2g_edges,
    edge_first,
    edge_second,
    edge_bias,
    edge_gain,
    node_first,
    node_second,
    node_bias,
    node_gain,
):
    table, mesh_three, gq, gp, picks, seconds = mesh_part(
        grid_nodes,
        mesh_nodes,
        grid_rim,
        mesh_rim,
        jnp.transpose(long_send, (0, 2, 1)),
        g2m_edges,
        short_edges,
        long_edges,
        jnp.transpose(m2g_edges, (1, 0, 2)),
        edge_first,
        edge_second,
        edge_bias,
        edge_gain,
        node_first,
        node_second,
        node_bias,
        node_gain,
    )
    grid_out, mesh_out = decode_part(
        owned_nodes,
        picks,
        table,
        gq,
        gp,
        grid_nodes,
        mesh_three,
        seconds,
        node_first,
        edge_gain,
        node_gain,
    )
    return (grid_out, mesh_out)


def solution(mesh):
    rows = P(("aa", "ba"), None)
    lists = P(("aa", "ba"), None, None)
    in_specs = (rows, rows, P(("aa", "ba"))) + (lists,) * 7 + (P(),) * 8
    return jax.shard_map(
        per_device, mesh=mesh, in_specs=in_specs, out_specs=(rows, rows), check_vma=False
    )
```

time: 87.7 us -> 75.9 us (0.87)
  Pallas kernels: 83.4 us -> 74.5 us
  local copies, waits for them, and re-layouts: 2.72 us -> 0 us
    pallas_call x1, Pallas kernels: 71.6 us -> 65 us  [mesh_part(): pl.pallas_call(mesh_kernel, name='mesh_part', in_specs=[anywhere] * 17, o...]
    unnamed x2 -> x0, local copies, waits for them, and re-layouts: 2.72 us -> none
    pallas_call x1, Pallas kernels: 11.9 us -> 9.45 us  [decode_part(): pl.pallas_call(decode_kernel, name='decode_part', grid=(G_DEV // DEC_TILE...]
where the time goes in v2:
time: 75.9 us; the launch traced here: 75.8 us
  Pallas kernels  74.5 us (98%)
  between operations  1.29 us (2%)
    pallas_call x1, Pallas kernels, mesh_part(): pl.pallas_call(mesh_kernel, name='mesh_part', in_specs=[anywhere] * 17, o...  65 us
    pallas_call x1, Pallas kernels, decode_part(): pl.pallas_call(decode_kernel, name='decode_part', grid=(G_DEV // DEC_TILE...  9.45 us

profile of v2, /device:TPU:0, one launch (start us, length us, event | category | flops | bytes accessed | tf_op | source)
XLA Modules:
  0.0 75.8 jit_solution(6976810698314306844)
XLA Ops:
  1.3 65.0 %mesh_part.1 = (bf16[384,512]{1,0:T(8,128)(2,1)}, bf16[192,512]{1,0:T(8,128)(2,1)}, bf16[1024,512]{1,0:T(8,128)(2,1)}, bf16[1024,512]{1,0:T(8,128)(2,1)}, bf16[3...) custom-call(bf16[1024,512]{1,0:T(8,128)(2,1)} %grid_rows.1, bf16[192,512]{1,0:T(8,128)(2,1)} %mesh_nodes.1, ...), custom_call_target="tpu_custom_call" | custom-call | tf_op jit(solution)/shard_map/mesh_part/pallas_call | solution.py:494
  66.3 9.4 %decode_part.1 = (bf16[1024,512]{1,0:T(8,128)(2,1)}, bf16[192,512]{1,0:T(8,128)(2,1)}) custom-call(s32[1]{0:T(128)S(6)} %copy.20.owned, bf16[3,1024,384]{2,1,0:T(8,128)(2,1)} %get-tuple-element.8.picks, bf16[384,512]{1,0:T(8,128)(2,1)} %get-tuple-element.9.table, bf16[1024,512]{1,0:T(8,128)(2,1)} %get-tuple-element.10.gq, ...), custom_call_target="tpu_custom_call" | custom-call | tf_op jit(solution)/shard_map/decode_part/pallas_call | solution.py:601

commit v3 on v2

--- a/solution.py
+++ b/solution.py
@@ -13,12 +13,16 @@
 HB = 16
 KL = 8
 CS = 16
+NOWHERE = 4095
+EARLY = 4
 N_AA = 8
 N_BA = 16
 DEVICES = 128
 E_G2M = 3072
 E_MESH = 1536
-TILE = 512
+TILE_LOCAL = 512
+TILE_ENC = 768
+TILE_MESH = 768
 ALONG_FIRST = (-1, -1, -1, 0, 0, 1, 1, 1)
 ALONG_SECOND = (-1, 0, 1, -1, 1, -1, 0, 1)
 F32 = jnp.float32
@@ -41,8 +45,7 @@
     return jnp.dot(a, b, preferred_element_type=F32)
 
 
-def silu(x):
-    half = (0.5 * x).astype(BF16)
+def silu_of_half(half):
     return half * jnp.tanh(half) + half
 
 
@@ -56,43 +59,62 @@
     return centred * lax.rsqrt(spread + EPSILON)
 
 
-def columns(row):
+def spread_out(row):
     parts = []
     for start in range(0, row.shape[1], 128):
-        part = row[:, start : start + 128].astype(F32)
-        parts.append(jnp.broadcast_to(part, (128, 128)).T)
+        parts.append(jnp.broadcast_to(row[:, start : start + 128], (128, 128)).T.astype(BF16))
     return parts[0] if len(parts) == 1 else jnp.concatenate(parts, 0)
 
 
-def split_ids(cols):
-    block = jnp.floor(cols * (1.0 / 256.0))
-    return block.astype(BF16), (cols - 256.0 * block).astype(BF16)
+def columns(row):
+    return spread_out((row >> 8).astype(F32)), spread_out((row & 255).astype(F32))
+
+
+def lane_ids(rows):
+    lane = lax.broadcasted_iota(jnp.int32, (rows, 128), 1).astype(F32)
+    return lane.astype(BF16), (lane + 128.0).astype(BF16)
 
 
 def one_hot(cols, first, width):
-    rows = cols.shape[0]
-    block, place = split_ids(cols)
-    lane = lax.broadcasted_iota(jnp.int32, (rows, 128), 1).astype(F32)
-    lanes = (lane.astype(BF16), (lane + 128.0).astype(BF16))
+    block, place = cols
+    lanes = lane_ids(place.shape[0])
     one, zero = jnp.ones((), BF16), jnp.zeros((), BF16)
     parts = []
     for start in range(first, first + width, 256):
-        here = jnp.where(block == jnp.asarray(start // 256, BF16), place, jnp.asarray(-1, BF16))
+        here = place
+        if block is not None:
+            here = jnp.where(block == jnp.asarray(start // 256, BF16), place, jnp.asarray(-1, BF16))
         for half in range(2):
             if start + 128 * half < first + width:
                 parts.append(jnp.where(here == lanes[half], one, zero))
     return parts[0] if len(parts) == 1 else jnp.concatenate(parts, 1)
 
 
+def double_one_hot(first, second, width):
+    lanes = lane_ids(first[1].shape[0])
+    one, zero, none = jnp.ones((), BF16), jnp.zeros((), BF16), jnp.asarray(-1, BF16)
+    parts = []
+    for start in range(0, width, 256):
+        group = jnp.asarray(start // 256, BF16)
+        one_here = jnp.where(first[0] == group, first[1], none)
+        two_here = jnp.where(second[0] == group, second[1], none)
+        for half in range(2):
+            if start + 128 * half < width:
+                found = (one_here == lanes[half]) | (two_here == lanes[half])
+                parts.append(jnp.where(found, one, zero))
+    return jnp.concatenate(parts, 1)
+
+
 def scatter_matrix(row):
-    slots = lax.broadcasted_iota(jnp.int32, (M_DEV, row.shape[1]), 0)
-    return jnp.where(slots == row, 1.0, 0.0).astype(BF16)
+    slots = lax.broadcasted_iota(jnp.int32, (M_DEV, row.shape[1]), 0).astype(F32).astype(BF16)
+    ids = row.astype(F32).astype(BF16)
+    return jnp.where(slots == ids, jnp.ones((), BF16), jnp.zeros((), BF16))
 
 
 def node_update(rows, totals, first_own, first_sum, bias, second, gain):
     pre = dot(rows, first_own) + dot(totals.astype(BF16), first_sum) + bias
-    hidden = silu(pre)
-    result = normalised(dot(hidden, second)) * gain
+    result = dot(silu_of_half((0.5 * pre).astype(BF16)), second)
+    result = normalised(result) * gain
     return (rows.astype(F32) + result).astype(BF16)
 
 
@@ -142,10 +164,10 @@
     enc_rim,
     partial,
     picks_v,
-    hidden_v,
     proj_v,
     coarse_v,
     rim_picks,
+    list_picks,
     short_table,
     short_rim,
     long_table,
@@ -206,6 +228,33 @@
     load("ef01", edge_first.at[0, 1], ef_v.at[0, 1])
     load("eb", edge_bias, eb_v)
     load("g2m", g2m_edges, g2m_v)
+    def halo_copy(k, sem_base, rim, table, first, depth):
+        return pltpu.make_async_remote_copy(
+            src_ref=rim.at[pl.ds(k * depth, depth)],
+            dst_ref=table.at[pl.ds(first + (7 - k) * depth, depth)],
+            send_sem=halo_send.at[sem_base + k],
+            recv_sem=halo_recv.at[sem_base + 7 - k],
+            device_id=at(ALONG_FIRST[k], ALONG_SECOND[k]),
+            device_id_type=MESH,
+        )
+
+    copies = []
+    arrived("grim", "grid")
+    for pair in ((5, 4), (3, 2), (7, 6), (1, 0)):
+        cols = columns(jnp.concatenate([grim_v[0, k : k + 1, :] for k in pair], 1))
+        rows = dot(one_hot(cols, 0, G_DEV), grid_v[...]).astype(BF16)
+        if not copies:
+            arrived("ef00")
+        rows = (0.5 * dot(rows, ef_v[0, 0])).astype(BF16)
+        for place, k in enumerate(pair):
+            enc_rim[k * GB : (k + 1) * GB, :] = rows[place * GB : (place + 1) * GB, :]
+        if not copies:
+            pl.semaphore_wait(barrier, 8)
+        for k in pair:
+            copy = halo_copy(k, 0, enc_rim, enc_halo, 0, GB)
+            copy.start()
+            copies.append((k, copy))
+    greet(spread_sem.at[0], 1, 1, range(8))
     load("es0", edge_second.at[0], es_v.at[0])
     load("ns0", node_second.at[0], ns_v.at[0])
     load("nf0", node_first.at[0], nf_v.at[0])
@@ -230,58 +279,42 @@
     load("ns3", node_second.at[3], ns_v.at[3])
     load("m2g", m2g_edges, m2g_v)
 
-    def halo_copy(k, sem_base, rim, table, first, depth):
-        return pltpu.make_async_remote_copy(
-            src_ref=rim.at[pl.ds(k * depth, depth)],
-            dst_ref=table.at[pl.ds(first + (7 - k) * depth, depth)],
-            send_sem=halo_send.at[sem_base + k],
-            recv_sem=halo_recv.at[sem_base + 7 - k],
-            device_id=at(ALONG_FIRST[k], ALONG_SECOND[k]),
-            device_id_type=MESH,
-        )
-
-    copies = []
-    arrived("grim", "grid")
-    for pair in ((3, 4), (0, 7), (2, 5), (1, 6)):
-        cols = jnp.concatenate([columns(grim_v[0, k : k + 1, :]) for k in pair], 0)
-        rows = dot(one_hot(cols, 0, G_DEV), grid_v[...]).astype(BF16)
-        if not copies:
-            arrived("ef00")
-        rows = dot(rows, ef_v[0, 0]).astype(BF16)
-        for place, k in enumerate(pair):
-            enc_rim[k * GB : (k + 1) * GB, :] = rows[place * GB : (place + 1) * GB, :]
-        if not copies:
-            pl.semaphore_wait(barrier, 8)
-        for k in pair:
-            copy = halo_copy(k, 0, enc_rim, enc_halo, 0, GB)
-            copy.start()
-            copies.append(copy)
-    greet(spread_sem.at[0], 1, 1, range(8))
-
     for start in range(0, G_DEV, 512):
-        enc_table[start : start + 512, :] = dot(grid_v[start : start + 512, :], ef_v[0, 0]).astype(BF16)
+        half = 0.5 * dot(grid_v[start : start + 512, :], ef_v[0, 0])
+        enc_table[start : start + 512, :] = half.astype(BF16)
     arrived("mesh", "ef01", "eb")
-    enc_table[G_DEV : G_DEV + M_DEV, :] = (dot(mesh_v[...], ef_v[0, 1]) + eb_v[0:1, :]).astype(BF16)
+    enc_table[G_DEV : G_DEV + M_DEV, :] = (0.5 * (dot(mesh_v[...], ef_v[0, 1]) + eb_v[0:1, :])).astype(BF16)
     enc_table[G_DEV + M_DEV : G_DEV + 256, :] = jnp.zeros((64, D), BF16)
     proj_v[M_DEV:256, :] = jnp.zeros((64, D), BF16)
     coarse_v[...] = jnp.zeros((128, D), BF16)
     arrived("g2m")
 
-    def enc_local(step, carry):
-        start = pl.multiple_of(step * TILE, TILE)
-        here = pl.ds(start, TILE)
-        senders = columns(g2m_v[0, 0:1, here])
+    def tile_of(index):
+        return pl.ds(index * TILE_LOCAL, TILE_LOCAL)
+
+    def near_picks(index):
+        here = tile_of(index)
+        block, place = columns(g2m_v[0, 0:1, here])
+        picks_v[here, :] = one_hot((block, place), G_DEV, 8 * GB)
         targets = columns(g2m_v[0, 1:2, here])
-        picks = jnp.concatenate([one_hot(senders, 0, G_DEV), one_hot(targets, 0, 256)], 1)
-        partial[here, :] = dot(picks, enc_table[...])
-        picks_v[here, :] = one_hot(senders, G_DEV, 8 * GB)
-        return carry
-
-    lax.fori_loop(0, E_G2M // TILE, enc_local, 0)
+        return jnp.concatenate([one_hot((block, place), 0, G_DEV), one_hot(targets, 0, 256)], 1)
+
+    tiles = E_G2M // TILE_LOCAL
+    picks = near_picks(0)
+    for index in range(tiles):
+        sums = dot(picks, enc_table[...])
+        if index + 1 < tiles:
+            picks = near_picks(index + 1)
+        partial[tile_of(index), :] = sums.astype(BF16)
 
     def centre(section):
-        es_v[section] = centred_weights(es_v[section])
-        ns_v[section] = centred_weights(ns_v[section])
+        def block(step, carry):
+            here = pl.ds(pl.multiple_of(step * 128, 128), 128)
+            es_v[section, here, :] = centred_weights(es_v[section, here, :])
+            ns_v[section, here, :] = centred_weights(ns_v[section, here, :])
+            return carry
+
+        lax.fori_loop(0, D // 128, block, 0)
 
     arrived("es0", "ns0")
     centre(0)
@@ -293,29 +326,23 @@
         row = jnp.broadcast_to(mrim_v[0, k : k + 1, :].astype(F32), (HB, HB))
         col = jnp.sum(jnp.where(sub == lane, row, 0.0), axis=1, keepdims=True)
         parts.append(jnp.broadcast_to(col, (HB, 128)))
-    rim_picks[...] = one_hot(jnp.concatenate(parts, 0), 0, 128)
-    arrived("es1", "ns1")
-    centre(1)
-
-    def produce(x):
-        hidden_v[...] = silu(x)
-
-    def consume(section, edges, start):
-        message = normalised(dot(hidden_v[...], es_v[section])).astype(BF16)
-        totals[...] += dot(scatter_matrix(edges[0, 1:2, pl.ds(start, TILE)]), message)
-
-    def rounds(section, edges, count, picked):
+    rim_picks[...] = one_hot((None, jnp.concatenate(parts, 0).astype(BF16)), 0, 128)
+    def rounds(section, tile, edges, count, picked):
         totals[...] = jnp.zeros((M_DEV, D), F32)
-        produce(picked(0))
-
-        def step(index, carry):
-            start = pl.multiple_of(index * TILE, TILE)
-            consume(section, edges, pl.multiple_of(start - TILE, TILE))
-            produce(picked(start))
-            return carry
-
-        lax.fori_loop(1, count, step, 0)
-        consume(section, edges, (count - 1) * TILE)
+        tiles = count // tile
+        hidden, result = {}, {}
+        for step in range(tiles + 2):
+            if step < tiles:
+                half = picked(step * tile)
+            if 0 <= step - 2:
+                message = normalised(result.pop(step - 2)).astype(BF16)
+            if 0 <= step - 1 < tiles:
+                result[step - 1] = dot(hidden.pop(step - 1), es_v[section])
+            if step < tiles:
+                hidden[step] = silu_of_half(half)
+            if 0 <= step - 2:
+                targets = edges[0, 1:2, (step - 2) * tile : (step - 1) * tile]
+                totals[...] += dot(scatter_matrix(targets), message)
 
     def updated(section, rows, sums):
         return node_update(
@@ -331,18 +358,29 @@
     arrived("nf0", "eg", "ng", "nb")
     pl.semaphore_wait(spread_sem.at[0], 8)
     greet(spread_sem.at[1], 2, 2, range(8))
-    for copy in copies:
-        copy.wait()
+
+    for k, copy in copies:
+        if 7 - k < EARLY:
+            copy.wait_recv()
+
+    for index in range(tiles):
+        here = tile_of(index)
+        partial[here, :] += dot(picks_v[here, 0 : EARLY * GB], enc_halo[0 : EARLY * GB, :]).astype(BF16)
+    for k, copy in copies:
+        copy.wait_send()
+        if 7 - k >= EARLY:
+            copy.wait_recv()
 
     def enc_picked(start):
-        here = pl.ds(start, TILE)
-        return partial[here, :] + dot(picks_v[here, :], enc_halo[...])
-
-    rounds(0, g2m_v, E_G2M // TILE, enc_picked)
+        here = pl.ds(start, TILE_ENC)
+        late = dot(picks_v[here, EARLY * GB :], enc_halo[EARLY * GB :, :])
+        return partial[here, :] + late.astype(BF16)
+
+    rounds(0, TILE_ENC, g2m_v, E_G2M, enc_picked)
     mesh_v[...] = updated(0, mesh_v[...], totals[...])
 
     def mesh_halo(section, sem_base, rim, table):
-        proj = dot(mesh_v[...], ef_v[section, 0]).astype(BF16)
+        proj = (0.5 * dot(mesh_v[...], ef_v[section, 0])).astype(BF16)
         proj_v[0:M_DEV, :] = proj
         rim[...] = dot(rim_picks[...], proj_v[0:128, :]).astype(BF16)
         started = []
@@ -355,48 +393,21 @@
 
     arrived("ef1")
     copies = mesh_halo(1, 8, short_rim, short_table)
-    short_table[M_DEV + 8 * HB : 512, :] = (dot(mesh_v[...], ef_v[1, 1]) + eb_v[1:2, :]).astype(BF16)
+    short_table[M_DEV + 8 * HB : 512, :] = (0.5 * (dot(mesh_v[...], ef_v[1, 1]) + eb_v[1:2, :])).astype(
+        BF16
+    )
     arrived("short")
 
-    def double_one_hot(first, second, width):
-        rows = first.shape[0]
-        one_block, one_place = split_ids(first)
-        two_block, two_place = split_ids(second)
-        lane = lax.broadcasted_iota(jnp.int32, (rows, 128), 1).astype(F32)
-        lanes = (lane.astype(BF16), (lane + 128.0).astype(BF16))
-        one, zero, none = jnp.ones((), BF16), jnp.zeros((), BF16), jnp.asarray(-1, BF16)
-        parts = []
-        for start in range(0, width, 128):
-            group = jnp.asarray(start // 256, BF16)
-            here = lanes[start // 128 % 2]
-            one_here = jnp.where(one_block == group, one_place, none)
-            two_here = jnp.where(two_block == group, two_place, none)
-            parts.append(jnp.where((one_here == here) | (two_here == here), one, zero))
-        return jnp.concatenate(parts, 1)
-
     def short_picks(step, carry):
-        here = pl.ds(pl.multiple_of(step * TILE, TILE), TILE)
+        here = pl.ds(pl.multiple_of(step * TILE_LOCAL, TILE_LOCAL), TILE_LOCAL)
         senders = columns(short_v[0, 0:1, here])
-        targets = columns(short_v[0, 1:2, here]) + float(M_DEV + 8 * HB)
+        targets = columns(short_v[0, 1:2, here] + (M_DEV + 8 * HB))
         picks_v[here, 0:512] = double_one_hot(senders, targets, 512)
         return carry
 
-    lax.fori_loop(0, E_MESH // TILE, short_picks, 0)
-    arrived("es2", "ns2", "nf1")
-    centre(2)
-    pl.semaphore_wait(spread_sem.at[1], 8)
-    greet(spread_sem.at[2], 0, 4, (3, 4))
-    for copy in copies:
-        copy.wait()
-
-    def short_picked(start):
-        return dot(picks_v[pl.ds(start, TILE), 0:512], short_table[...])
-
-    rounds(1, short_v, E_MESH // TILE, short_picked)
-
-    arrived("ef2", "send")
-    coarse = updated(1, mesh_v[0:CS, :], totals[0:CS, :])
-    coarse_v[0:CS, :] = dot(coarse, ef_v[2, 0]).astype(BF16)
+    lax.fori_loop(0, E_MESH // TILE_LOCAL, short_picks, 0)
+    arrived("es1", "ns1", "nf1", "send")
+    centre(1)
     lists = send_v[0].astype(F32).astype(BF16)
     for start in range(0, DEVICES * KL, 512):
         sub = lax.broadcasted_iota(jnp.int32, (512, DEVICES), 0) + start
@@ -406,7 +417,24 @@
         sub = lax.broadcasted_iota(jnp.int32, (512, KL), 0)
         lane = lax.broadcasted_iota(jnp.int32, (512, KL), 1)
         col = jnp.sum(jnp.where(lax.rem(sub, KL) == lane, listed, 0.0), axis=1, keepdims=True)
-        rows = dot(one_hot(jnp.broadcast_to(col, (512, 128)), 0, 128), coarse_v[...])
+        list_picks[start : start + 512, :] = one_hot(
+            (None, jnp.broadcast_to(col, (512, 128)).astype(BF16)), 0, 128
+        )
+    pl.semaphore_wait(spread_sem.at[1], 8)
+    greet(spread_sem.at[2], 0, 4, (3, 4))
+    for copy in copies:
+        copy.wait()
+
+    def short_picked(start):
+        return dot(picks_v[pl.ds(start, TILE_MESH), 0:512], short_table[...]).astype(BF16)
+
+    rounds(1, TILE_MESH, short_v, E_MESH, short_picked)
+
+    arrived("ef2")
+    coarse = updated(1, mesh_v[0:CS, :], totals[0:CS, :])
+    coarse_v[0:CS, :] = (0.5 * dot(coarse, ef_v[2, 0])).astype(BF16)
+    for start in range(0, DEVICES * KL, 512):
+        rows = dot(list_picks[start : start + 512, :], coarse_v[...])
         long_out[start // KL : (start + 512) // KL] = rows.reshape(512 // KL, KL, D).astype(BF16)
     pl.semaphore_wait(spread_sem.at[2], 2)
     for first, second in PEERS:
@@ -423,26 +451,28 @@
     long_in[me] = long_out[me]
 
     mesh_v[...] = updated(1, mesh_v[...], totals[...])
-    long_table[0:M_DEV, :] = dot(mesh_v[...], ef_v[2, 0]).astype(BF16)
-    long_table[M_DEV : 2 * M_DEV, :] = (dot(mesh_v[...], ef_v[2, 1]) + eb_v[2:3, :]).astype(BF16)
+    long_table[0:M_DEV, :] = (0.5 * dot(mesh_v[...], ef_v[2, 0])).astype(BF16)
+    long_table[M_DEV : 2 * M_DEV, :] = (0.5 * (dot(mesh_v[...], ef_v[2, 1]) + eb_v[2:3, :])).astype(BF16)
     arrived("long")
 
     def long_local(step, carry):
-        here = pl.ds(pl.multiple_of(step * TILE, TILE), TILE)
-        senders = columns(long_v[0, 0:1, here])
-        own = jnp.where(senders < float(M_DEV), senders, -1.0)
-        targets = columns(long_v[0, 1:2, here]) + float(M_DEV)
-        partial[here, :] = dot(double_one_hot(own, targets, 2 * M_DEV), long_table[...])
-        away = jnp.where(senders < float(M_DEV), -1.0, senders - float(M_DEV))
+        here = pl.ds(pl.multiple_of(step * TILE_LOCAL, TILE_LOCAL), TILE_LOCAL)
+        senders = long_v[0, 0:1, here]
+        own = columns(jnp.where(senders < M_DEV, senders, NOWHERE))
+        targets = columns(long_v[0, 1:2, here] + M_DEV)
+        sums = dot(double_one_hot(own, targets, 2 * M_DEV), long_table[...])
+        partial[here, :] = sums.astype(BF16)
+        away = columns(jnp.where(senders < M_DEV, NOWHERE, senders - M_DEV))
         picks_v[here, :] = one_hot(away, 0, DEVICES * KL)
         return carry
 
-    lax.fori_loop(0, E_MESH // TILE, long_local, 0)
-    arrived("ef3", "nf30", "es3", "ns3", "m2g")
+    lax.fori_loop(0, E_MESH // TILE_LOCAL, long_local, 0)
+    arrived("ef3", "nf30", "es2", "ns2", "es3", "ns3", "m2g")
+    centre(2)
     for start in range(0, G_DEV, 512):
         rows = grid_v[start : start + 512, :]
-        gq_v[start : start + 512, :] = (dot(rows, ef_v[3, 1]) + eb_v[3:4, :]).astype(BF16)
-        gp_v[start : start + 512, :] = (dot(rows, nf_v[3, 0]) + nb_v[3:4, :]).astype(BF16)
+        gq_v[start : start + 512, :] = (0.5 * (dot(rows, ef_v[3, 1]) + eb_v[3:4, :])).astype(BF16)
+        gp_v[start : start + 512, :] = (0.5 * (dot(rows, nf_v[3, 0]) + nb_v[3:4, :])).astype(BF16)
     centre(3)
     gq_copy = pltpu.make_async_copy(gq_v, gq_out, out_sem.at[0])
     gp_copy = pltpu.make_async_copy(gp_v, gp_out, out_sem.at[1])
@@ -469,10 +499,10 @@
         long_rows[start * KL : (start + 32) * KL, :] = block.astype(BF16)
 
     def long_picked(start):
-        here = pl.ds(start, TILE)
-        return partial[here, :] + dot(picks_v[here, :], long_rows[...])
-
-    rounds(2, long_v, E_MESH // TILE, long_picked)
+        here = pl.ds(start, TILE_MESH)
+        return partial[here, :] + dot(picks_v[here, :], long_rows[...]).astype(BF16)
+
+    rounds(2, TILE_MESH, long_v, E_MESH, long_picked)
     mesh_v[...] = updated(2, mesh_v[...], totals[...])
 
     copies = mesh_halo(3, 16, dec_rim, dec_table)
@@ -525,12 +555,12 @@
             vmem((G_DEV + 256, D), BF16),
             vmem((8 * GB, D), BF16),
             vmem((8 * GB, D), BF16),
-            vmem((E_G2M, D), F32),
+            vmem((E_G2M, D), BF16),
             vmem((E_G2M, 8 * GB), BF16),
-            vmem((TILE, D), BF16),
             vmem((256, D), BF16),
             vmem((128, D), BF16),
             vmem((128, 128), BF16),
+            vmem((DEVICES * KL, 128), BF16),
             vmem((512, D), BF16),
             vmem((8 * HB, D), BF16),
             vmem((2 * M_DEV, D), BF16),
@@ -558,6 +588,7 @@
 
 
 DEC_TILE = 256
+DEC_ROWS = 512
 
 
 def decode_kernel(
@@ -574,53 +605,141 @@
     node_gain,
     grid_out,
     mesh_out,
+    picks_v,
+    total_v,
+    table_v,
+    gq_v,
+    gp_v,
+    grid_v,
+    mesh_v,
+    second_v,
+    sum_v,
+    eg_v,
+    ng_v,
+    in_sem,
+    out_sem,
 ):
-    @pl.when(pl.program_id(0) == 0)
-    def _():
-        slot = lax.broadcasted_iota(jnp.int32, (M_DEV, D), 0)
-        mesh_out[...] = jnp.where(slot < owned[0], mesh_rows[...].astype(F32), 0.0).astype(BF16)
-
-    target = gq[...].astype(F32)
-    x = dot(picks[...].reshape(3 * DEC_TILE, 384), table[...])
-    hidden = silu(x + jnp.concatenate([target] * 3, 0))
-    message = normalised(dot(hidden, seconds[0]))
-    total = message[0:DEC_TILE] + message[DEC_TILE : 2 * DEC_TILE] + message[2 * DEC_TILE :]
-    total = total * edge_gain[3:4, :]
-    pre = gp[...].astype(F32) + dot(total.astype(BF16), node_sum[0, 0])
-    result = normalised(dot(silu(pre), seconds[1])) * node_gain[3:4, :]
-    grid_out[...] = (grid_rows[...].astype(F32) + result).astype(BF16)
-
-
-def decode_part(owned, picks, table, gq, gp, grid_rows, mesh_rows, seconds, nf, eg, ng):
-    def whole(*shape):
-        return pl.BlockSpec(shape, lambda i: (0,) * len(shape))
-
-    def tiled():
-        return pl.BlockSpec((DEC_TILE, D), lambda i: (i, 0))
-
+    tiles = G_DEV // DEC_TILE
+    loads = {}
+
+    def load(name, src, dst):
+        copy = pltpu.make_async_copy(src, dst, in_sem.at[len(loads)])
+        copy.start()
+        loads[name] = copy
+
+    def part(index):
+        return pl.ds(index * DEC_TILE, DEC_TILE)
+
+    load("table", table, table_v)
+    for t in range(tiles):
+        load(("picks", t), picks.at[:, part(t)], picks_v.at[:, part(t)])
+        load(("gq", t), gq.at[part(t)], gq_v.at[part(t)])
+        if t == 0:
+            load("es", seconds.at[0], second_v.at[0])
+            load("eg", edge_gain, eg_v)
+    load("nf", node_sum.at[3, 1], sum_v)
+    load("ns", seconds.at[1], second_v.at[1])
+    load("ng", node_gain, ng_v)
+    for t in range(tiles):
+        load(("gp", t), gp.at[part(t)], gp_v.at[part(t)])
+        load(("grid", t), grid_rows.at[part(t)], grid_v.at[part(t)])
+    load("mesh", mesh_rows, mesh_v)
+    outs = []
+    hidden, result, node, update = {}, {}, {}, {}
+
+    def rows_of(index):
+        return pl.ds(index * DEC_ROWS, DEC_ROWS)
+
+    blocks = G_DEV // DEC_ROWS
+    first_block = DEC_ROWS // DEC_TILE + 2
+
+    def node_start(t):
+        if t == 0:
+            for name in ("nf", "ns", "ng"):
+                loads[name].wait()
+        for index in range(t * DEC_ROWS // DEC_TILE, (t + 1) * DEC_ROWS // DEC_TILE):
+            loads["gp", index].wait()
+            loads["grid", index].wait()
+        return (0.5 * dot(total_v[rows_of(t), :], sum_v[...])).astype(BF16)
+
+    def node_end(t):
+        rows = grid_v[rows_of(t), :].astype(F32) + normalised(update.pop(t)) * ng_v[3:4, :]
+        grid_v[rows_of(t), :] = rows.astype(BF16)
+        outs.append(
+            pltpu.make_async_copy(grid_v.at[rows_of(t)], grid_out.at[rows_of(t)], out_sem.at[t])
+        )
+        outs[-1].start()
+
+    loads["table"].wait()
+    gap = DEC_ROWS // DEC_TILE
+    for step in range(first_block + gap * (blocks - 1) + 3):
+        if step < tiles:
+            loads["picks", step].wait()
+            loads["gq", step].wait()
+            picked = dot(picks_v[:, part(step), :].reshape(3 * DEC_TILE, 384), table_v[...]).astype(BF16)
+        t = step - 2
+        if 0 <= t < tiles:
+            message = normalised(result.pop(t))
+            summed = message[0:DEC_TILE] + message[DEC_TILE : 2 * DEC_TILE] + message[2 * DEC_TILE :]
+            total_v[part(t), :] = (summed * eg_v[3:4, :]).astype(BF16)
+        t = step - 1
+        if 0 <= t < tiles:
+            if t == 0:
+                loads["es"].wait()
+                loads["eg"].wait()
+            result[t] = dot(hidden.pop(t), second_v[0])
+        block, phase = divmod(step - first_block, gap) if gap > 1 else (step - first_block, 0)
+        starts = phase == 0 and 0 <= block < blocks
+        if starts:
+            pre = node_start(block)
+        if step < tiles:
+            hidden[step] = silu_of_half(picked + jnp.concatenate([gq_v[part(step), :]] * 3, 0))
+        for t in list(update):
+            node_end(t)
+        for t in list(node):
+            update[t] = dot(node.pop(t), second_v[1])
+        if starts:
+            node[block] = silu_of_half(pre + gp_v[rows_of(block), :])
+        if step == tiles:
+            loads["mesh"].wait()
+            slot = lax.broadcasted_iota(jnp.int32, (M_DEV, D), 0)
+            mesh_v[...] = jnp.where(slot < owned[0], mesh_v[...].astype(F32), 0.0).astype(BF16)
+            outs.append(pltpu.make_async_copy(mesh_v, mesh_out, out_sem.at[tiles]))
+            outs[-1].start()
+    for copy in outs:
+        copy.wait()
+
+
+def decode_part(*operands):
+    vmem = pltpu.VMEM
+    anywhere = pl.BlockSpec(memory_space=pl.ANY)
+    tiles = G_DEV // DEC_TILE
     return pl.pallas_call(
         decode_kernel,
         name="decode_part",
-        grid=(G_DEV // DEC_TILE,),
-        in_specs=[
-            pl.BlockSpec(memory_space=pltpu.SMEM),
-            pl.BlockSpec((3, DEC_TILE, 384), lambda i: (0, i, 0)),
-            whole(384, D),
-            tiled(),
-            tiled(),
-            tiled(),
-            whole(M_DEV, D),
-            whole(2, D, D),
-            pl.BlockSpec((1, 1, D, D), lambda i: (3, 1, 0, 0)),
-            whole(4, D),
-            whole(4, D),
-        ],
-        out_specs=[tiled(), whole(M_DEV, D)],
+        in_specs=[pl.BlockSpec(memory_space=pltpu.SMEM)] + [anywhere] * 10,
+        out_specs=[anywhere] * 2,
         out_shape=[
             jax.ShapeDtypeStruct((G_DEV, D), BF16),
             jax.ShapeDtypeStruct((M_DEV, D), BF16),
         ],
-    )(owned, picks, table, gq, gp, grid_rows, mesh_rows, seconds, nf, eg, ng)
+        scratch_shapes=[
+            vmem((3, G_DEV, 384), BF16),
+            vmem((G_DEV, D), BF16),
+            vmem((384, D), BF16),
+            vmem((G_DEV, D), BF16),
+            vmem((G_DEV, D), BF16),
+            vmem((G_DEV, D), BF16),
+            vmem((M_DEV, D), BF16),
+            vmem((2, D, D), BF16),
+            vmem((D, D), BF16),
+            vmem((4, D), F32),
+            vmem((4, D), F32),
+            pltpu.SemaphoreType.DMA((8 + 4 * tiles,)),
+            pltpu.SemaphoreType.DMA((tiles + 1,)),
+        ],
+        compiler_params=pltpu.CompilerParams(vmem_limit_bytes=60 * 1024 * 1024),
+    )(*operands)
 
 
 def per_device(

time: 75.9 us -> 69.2 us (0.912)
  Pallas kernels: 74.5 us -> 67.6 us
    pallas_call x1, Pallas kernels: 65 us -> 58.9 us  [mesh_part(): pl.pallas_call(mesh_kernel, name='mesh_part', in_specs=[anywhere] * 17, o...]
where the time goes in v3:
time: 69.2 us; the launch traced here: 69.1 us
  Pallas kernels  67.6 us (98%)
  between operations  1.47 us (2%)
    pallas_call x1, Pallas kernels, mesh_part(): pl.pallas_call(mesh_kernel, name='mesh_part', in_specs=[anywhere] * 17, o...  58.9 us
    pallas_call x1, Pallas kernels, decode_part(): pl.pallas_call(decode_kernel, name='decode_part', in_specs=[pl.BlockSpec(...  8.71 us

profile of v3, /device:TPU:0, one launch (start us, length us, event | category | flops | bytes accessed | tf_op | source)
XLA Modules:
  0.0 69.1 jit_solution(5225751734126771933)
XLA Ops:
  1.3 58.9 %mesh_part.1 = (bf16[384,512]{1,0:T(8,128)(2,1)}, bf16[192,512]{1,0:T(8,128)(2,1)}, bf16[1024,512]{1,0:T(8,128)(2,1)}, bf16[1024,512]{1,0:T(8,128)(2,1)}, bf16[3...) custom-call(bf16[1024,512]{1,0:T(8,128)(2,1)} %grid_rows.1, bf16[192,512]{1,0:T(8,128)(2,1)} %mesh_nodes.1, ...), custom_call_target="tpu_custom_call" | custom-call | tf_op jit(solution)/shard_map/mesh_part/pallas_call | solution.py:524
  60.2 8.7 %decode_part.1 = (bf16[1024,512]{1,0:T(8,128)(2,1)}, bf16[192,512]{1,0:T(8,128)(2,1)}) custom-call(s32[1]{0:T(128)S(6)} %copy.20.owned, bf16[3,1024,384]{2,1,0:T(8,128)(2,1)} %get-tuple-element.8.picks, bf16[384,512]{1,0:T(8,128)(2,1)} %get-tuple-element.9.table, bf16[1024,512]{1,0:T(8,128)(2,1)} %get-tuple-element.10.gq, ...), custom_call_target="tpu_custom_call" | custom-call | tf_op jit(solution)/shard_map/decode_part/pallas_call | solution.py:717

commit v4 on v3

--- a/solution.py
+++ b/solution.py
@@ -35,9 +35,10 @@
     return sum(min(step, 4 - step) for step in steps)
 
 
+GROUP_ORDER = (2, 1, 3, 0)
 PEERS = sorted(
     [(a, b) for a in range(N_AA) for b in range(N_BA) if (a, b) != (0, 0)],
-    key=lambda peer: -hops(*peer),
+    key=lambda peer: (GROUP_ORDER.index(peer[1] // 4), -hops(*peer)),
 )
 
 
@@ -174,9 +175,11 @@
     long_out,
     long_in,
     long_rows,
-    dec_table,
+    dec_halo,
     dec_rim,
     dec_picks,
+    dec_near,
+    dec_sums,
     totals,
     gq_v,
     gp_v,
@@ -379,20 +382,21 @@
     rounds(0, TILE_ENC, g2m_v, E_G2M, enc_picked)
     mesh_v[...] = updated(0, mesh_v[...], totals[...])
 
-    def mesh_halo(section, sem_base, rim, table):
+    def mesh_halo(section, sem_base, rim, table, first):
         proj = (0.5 * dot(mesh_v[...], ef_v[section, 0])).astype(BF16)
         proj_v[0:M_DEV, :] = proj
         rim[...] = dot(rim_picks[...], proj_v[0:128, :]).astype(BF16)
         started = []
         for k in range(8):
-            copy = halo_copy(k, sem_base, rim, table, M_DEV, HB)
+            copy = halo_copy(k, sem_base, rim, table, first, HB)
             copy.start()
             started.append(copy)
-        table[0:M_DEV, :] = proj
+        if first:
+            table[0:first, :] = proj
         return started
 
     arrived("ef1")
-    copies = mesh_halo(1, 8, short_rim, short_table)
+    copies = mesh_halo(1, 8, short_rim, short_table, M_DEV)
     short_table[M_DEV + 8 * HB : 512, :] = (0.5 * (dot(mesh_v[...], ef_v[1, 1]) + eb_v[1:2, :])).astype(
         BF16
     )
@@ -440,15 +444,17 @@
     for first, second in PEERS:
         peer_first = lax.rem(band + first, N_AA)
         peer_second = (sector // 4 + second // 4) % 4 * 4 + (sector + second) % 4
+        group = -(second // 4) % 4
+        slot = group * 32 + -first % N_AA * 4 + -second % 4
         pltpu.make_async_remote_copy(
             src_ref=long_out.at[peer_first * N_BA + peer_second],
-            dst_ref=long_in.at[me],
+            dst_ref=long_in.at[slot],
             send_sem=long_ssem,
-            recv_sem=long_rsem,
+            recv_sem=long_rsem.at[group],
             device_id=(peer_first, peer_second),
             device_id_type=MESH,
         ).start()
-    long_in[me] = long_out[me]
+    long_in[0] = long_out[me]
 
     mesh_v[...] = updated(1, mesh_v[...], totals[...])
     long_table[0:M_DEV, :] = (0.5 * dot(mesh_v[...], ef_v[2, 0])).astype(BF16)
@@ -462,7 +468,11 @@
         targets = columns(long_v[0, 1:2, here] + M_DEV)
         sums = dot(double_one_hot(own, targets, 2 * M_DEV), long_table[...])
         partial[here, :] = sums.astype(BF16)
-        away = columns(jnp.where(senders < M_DEV, NOWHERE, senders - M_DEV))
+        far = jnp.maximum(senders - M_DEV, 0)
+        peer = far >> 3
+        slot = (((peer >> 2) - (sector >> 2)) & 3) * 32
+        slot = slot + (((peer >> 4) - band) & 7) * 4 + ((peer - sector) & 3)
+        away = columns(jnp.where(senders < M_DEV, NOWHERE, slot * KL + (far & 7)))
         picks_v[here, :] = one_hot(away, 0, DEVICES * KL)
         return carry
 
@@ -474,16 +484,18 @@
         gq_v[start : start + 512, :] = (0.5 * (dot(rows, ef_v[3, 1]) + eb_v[3:4, :])).astype(BF16)
         gp_v[start : start + 512, :] = (0.5 * (dot(rows, nf_v[3, 0]) + nb_v[3:4, :])).astype(BF16)
     centre(3)
-    gq_copy = pltpu.make_async_copy(gq_v, gq_out, out_sem.at[0])
     gp_copy = pltpu.make_async_copy(gp_v, gp_out, out_sem.at[1])
     es_copy = pltpu.make_async_copy(es_v.at[3], second_out.at[0], out_sem.at[2])
     ns_copy = pltpu.make_async_copy(ns_v.at[3], second_out.at[1], out_sem.at[3])
-    outs = [gq_copy, gp_copy, es_copy, ns_copy]
+    outs = [gp_copy, es_copy, ns_copy]
 
     def dec_ids(step, carry):
         here = pl.ds(pl.multiple_of(step * 512, 512), 512)
         for k in range(3):
-            dec_picks[k, here, :] = one_hot(columns(m2g_v[k, :, here]), 0, 384)
+            senders = m2g_v[k, :, here]
+            dec_near[k, here, :] = one_hot(columns(senders), 0, 256)
+            rims = jnp.where(senders < M_DEV, NOWHERE, senders - M_DEV)
+            dec_picks[k, here, :] = one_hot(columns(rims), 0, 128)
         return carry
 
     lax.fori_loop(0, G_DEV // 512, dec_ids, 0)
@@ -491,31 +503,50 @@
     for copy in outs:
         copy.start()
     arrived("nf2")
+    def long_arrived(group):
+        first = 1 if group == 0 else group * 32
+        blocks = long_in.at[pl.ds(first, (group + 1) * 32 - first)]
+        pltpu.make_async_copy(blocks, blocks, long_rsem.at[group]).wait()
+        rows = long_in[group * 32 : (group + 1) * 32].astype(F32).reshape(32 * KL, D)
+        long_rows[group * 256 : (group + 1) * 256, :] = rows.astype(BF16)
+
+    for group in (2, 3, 1):
+        long_arrived(group)
+        some = pl.ds(group * 256, 256)
+        for index in range(E_MESH // TILE_LOCAL):
+            here = tile_of(index)
+            partial[here, :] += dot(picks_v[here, some], long_rows[some, :]).astype(BF16)
     others = pl.ds(0, DEVICES - 1)
     pltpu.make_async_copy(long_out.at[others], long_out.at[others], long_ssem).wait()
-    pltpu.make_async_copy(long_in.at[others], long_in.at[others], long_rsem).wait()
-    for start in range(0, DEVICES, 32):
-        block = long_in[start : start + 32].astype(F32).reshape(32 * KL, D)
-        long_rows[start * KL : (start + 32) * KL, :] = block.astype(BF16)
+    long_arrived(0)
 
     def long_picked(start):
         here = pl.ds(start, TILE_MESH)
-        return partial[here, :] + dot(picks_v[here, :], long_rows[...]).astype(BF16)
+        return partial[here, :] + dot(picks_v[here, 0:256], long_rows[0:256, :]).astype(BF16)
 
     rounds(2, TILE_MESH, long_v, E_MESH, long_picked)
     mesh_v[...] = updated(2, mesh_v[...], totals[...])
 
-    copies = mesh_halo(3, 16, dec_rim, dec_table)
-    dec_table[M_DEV + 8 * HB : 384, :] = jnp.zeros((64, D), BF16)
+    copies = mesh_halo(3, 16, dec_rim, dec_halo, 0)
     outs.append(pltpu.make_async_copy(mesh_v, mesh_out, out_sem.at[5]))
+    outs[-1].start()
+    for half in range(2):
+        for k in range(3):
+            here = pl.ds(half * 512, 512)
+            sums = dot(dec_near[k, here, :], proj_v[...]).astype(BF16)
+            dec_sums[k, here, :] = sums + gq_v[here, :]
+            outs.append(
+                pltpu.make_async_copy(
+                    dec_sums.at[k, here], gq_out.at[k, here], out_sem.at[7 + 3 * half + k]
+                )
+            )
+            outs[-1].start()
+    for copy in copies:
+        copy.wait()
+    outs.append(pltpu.make_async_copy(dec_halo, dec_out, out_sem.at[6]))
     outs[-1].start()
     for copy in outs:
         copy.wait()
-    for copy in copies:
-        copy.wait()
-    dec_copy = pltpu.make_async_copy(dec_table, dec_out, out_sem.at[6])
-    dec_copy.start()
-    dec_copy.wait()
 
 
 def mesh_part(*operands):
@@ -527,11 +558,11 @@
         in_specs=[anywhere] * 17,
         out_specs=[anywhere] * 6,
         out_shape=[
-            jax.ShapeDtypeStruct((384, D), BF16),
+            jax.ShapeDtypeStruct((8 * HB, D), BF16),
             jax.ShapeDtypeStruct((M_DEV, D), BF16),
+            jax.ShapeDtypeStruct((3, G_DEV, D), BF16),
             jax.ShapeDtypeStruct((G_DEV, D), BF16),
-            jax.ShapeDtypeStruct((G_DEV, D), BF16),
-            jax.ShapeDtypeStruct((3, G_DEV, 384), BF16),
+            jax.ShapeDtypeStruct((3, G_DEV, 128), BF16),
             jax.ShapeDtypeStruct((2, D, D), BF16),
         ],
         scratch_shapes=[
@@ -567,18 +598,20 @@
             vmem((DEVICES, KL, D), BF16),
             vmem((DEVICES, KL, D), BF16),
             vmem((DEVICES * KL, D), BF16),
-            vmem((384, D), BF16),
             vmem((8 * HB, D), BF16),
-            vmem((3, G_DEV, 384), BF16),
+            vmem((8 * HB, D), BF16),
+            vmem((3, G_DEV, 128), BF16),
+            vmem((3, G_DEV, 256), BF16),
+            vmem((3, G_DEV, D), BF16),
             vmem((M_DEV, D), F32),
             vmem((G_DEV, D), BF16),
             vmem((G_DEV, D), BF16),
             pltpu.SemaphoreType.DMA((30,)),
-            pltpu.SemaphoreType.DMA((7,)),
+            pltpu.SemaphoreType.DMA((13,)),
             pltpu.SemaphoreType.DMA((24,)),
             pltpu.SemaphoreType.DMA((24,)),
             pltpu.SemaphoreType.DMA,
-            pltpu.SemaphoreType.DMA,
+            pltpu.SemaphoreType.DMA((4,)),
             pltpu.SemaphoreType.REGULAR((3,)),
         ],
         compiler_params=pltpu.CompilerParams(
@@ -587,15 +620,14 @@
     )(*operands)
 
 
-DEC_TILE = 256
-DEC_ROWS = 512
+DEC_TILE = 512
 
 
 def decode_kernel(
     owned,
     picks,
-    table,
-    gq,
+    halo,
+    sums,
     gp,
     grid_rows,
     mesh_rows,
@@ -606,9 +638,10 @@
     grid_out,
     mesh_out,
     picks_v,
+    halo_v,
+    sums_v,
+    added_v,
     total_v,
-    table_v,
-    gq_v,
     gp_v,
     grid_v,
     mesh_v,
@@ -619,7 +652,6 @@
     in_sem,
     out_sem,
 ):
-    tiles = G_DEV // DEC_TILE
     loads = {}
 
     def load(name, src, dst):
@@ -627,84 +659,78 @@
         copy.start()
         loads[name] = copy
 
-    def part(index):
-        return pl.ds(index * DEC_TILE, DEC_TILE)
-
-    load("table", table, table_v)
-    for t in range(tiles):
-        load(("picks", t), picks.at[:, part(t)], picks_v.at[:, part(t)])
-        load(("gq", t), gq.at[part(t)], gq_v.at[part(t)])
-        if t == 0:
+    order = [(half, k) for half in range(2) for k in range(3)]
+
+    def rows_of(half):
+        return pl.ds(half * DEC_TILE, DEC_TILE)
+
+    load("halo", halo, halo_v)
+    for half, k in order:
+        here = rows_of(half)
+        load(("picks", half, k), picks.at[k, here], picks_v.at[k, here])
+        load(("sums", half, k), sums.at[k, here], sums_v.at[k, here])
+        if half == 0 and k == 0:
             load("es", seconds.at[0], second_v.at[0])
             load("eg", edge_gain, eg_v)
     load("nf", node_sum.at[3, 1], sum_v)
     load("ns", seconds.at[1], second_v.at[1])
     load("ng", node_gain, ng_v)
-    for t in range(tiles):
-        load(("gp", t), gp.at[part(t)], gp_v.at[part(t)])
-        load(("grid", t), grid_rows.at[part(t)], grid_v.at[part(t)])
+    load("gp", gp, gp_v)
+    load("grid", grid_rows, grid_v)
     load("mesh", mesh_rows, mesh_v)
     outs = []
     hidden, result, node, update = {}, {}, {}, {}
-
-    def rows_of(index):
-        return pl.ds(index * DEC_ROWS, DEC_ROWS)
-
-    blocks = G_DEV // DEC_ROWS
-    first_block = DEC_ROWS // DEC_TILE + 2
-
-    def node_start(t):
-        if t == 0:
-            for name in ("nf", "ns", "ng"):
-                loads[name].wait()
-        for index in range(t * DEC_ROWS // DEC_TILE, (t + 1) * DEC_ROWS // DEC_TILE):
-            loads["gp", index].wait()
-            loads["grid", index].wait()
-        return (0.5 * dot(total_v[rows_of(t), :], sum_v[...])).astype(BF16)
-
-    def node_end(t):
-        rows = grid_v[rows_of(t), :].astype(F32) + normalised(update.pop(t)) * ng_v[3:4, :]
-        grid_v[rows_of(t), :] = rows.astype(BF16)
+    starts = {5: [(0, 512)], 8: [(512, 256), (768, 256)]}
+
+    def finish(first, count):
+        here = pl.ds(first, count)
+        rows = grid_v[here, :].astype(F32) + normalised(update.pop((first, count))) * ng_v[3:4, :]
+        grid_v[here, :] = rows.astype(BF16)
         outs.append(
-            pltpu.make_async_copy(grid_v.at[rows_of(t)], grid_out.at[rows_of(t)], out_sem.at[t])
+            pltpu.make_async_copy(grid_v.at[here], grid_out.at[here], out_sem.at[len(outs)])
         )
         outs[-1].start()
 
-    loads["table"].wait()
-    gap = DEC_ROWS // DEC_TILE
-    for step in range(first_block + gap * (blocks - 1) + 3):
-        if step < tiles:
-            loads["picks", step].wait()
-            loads["gq", step].wait()
-            picked = dot(picks_v[:, part(step), :].reshape(3 * DEC_TILE, 384), table_v[...]).astype(BF16)
-        t = step - 2
-        if 0 <= t < tiles:
-            message = normalised(result.pop(t))
-            summed = message[0:DEC_TILE] + message[DEC_TILE : 2 * DEC_TILE] + message[2 * DEC_TILE :]
-            total_v[part(t), :] = (summed * eg_v[3:4, :]).astype(BF16)
-        t = step - 1
-        if 0 <= t < tiles:
-            if t == 0:
+    loads["halo"].wait()
+    for step in range(11):
+        if step < 6:
+            half, k = order[step]
+            loads["picks", half, k].wait()
+            loads["sums", half, k].wait()
+            picked = dot(picks_v[k, rows_of(half), :], halo_v[...]).astype(BF16)
+        if 0 <= step - 2 < 6:
+            before, part = order[step - 2]
+            message = normalised(result.pop(step - 2))
+            if part == 0:
+                added_v[...] = message
+            elif part == 1:
+                added_v[...] += message
+            else:
+                total_v[rows_of(before), :] = ((added_v[...] + message) * eg_v[3:4, :]).astype(BF16)
+        if 0 <= step - 1 < 6:
+            if step == 1:
                 loads["es"].wait()
                 loads["eg"].wait()
-            result[t] = dot(hidden.pop(t), second_v[0])
-        block, phase = divmod(step - first_block, gap) if gap > 1 else (step - first_block, 0)
-        starts = phase == 0 and 0 <= block < blocks
-        if starts:
-            pre = node_start(block)
-        if step < tiles:
-            hidden[step] = silu_of_half(picked + jnp.concatenate([gq_v[part(step), :]] * 3, 0))
-        for t in list(update):
-            node_end(t)
-        for t in list(node):
-            update[t] = dot(node.pop(t), second_v[1])
-        if starts:
-            node[block] = silu_of_half(pre + gp_v[rows_of(block), :])
-        if step == tiles:
+            result[step - 1] = dot(hidden.pop(step - 1), second_v[0])
+        if step == 5:
+            for name in ("nf", "ns", "ng", "gp", "grid"):
+                loads[name].wait()
+        pres = {}
+        for block in starts.get(step, ()):
+            pres[block] = (0.5 * dot(total_v[pl.ds(*block), :], sum_v[...])).astype(BF16)
+        if step < 6:
+            hidden[step] = silu_of_half(picked + sums_v[k, rows_of(half), :])
+        for block in list(update):
+            finish(*block)
+        for block in list(node):
+            update[block] = dot(node.pop(block), second_v[1])
+        for block, pre in pres.items():
+            node[block] = silu_of_half(pre + gp_v[pl.ds(*block), :])
+        if step == 6:
             loads["mesh"].wait()
             slot = lax.broadcasted_iota(jnp.int32, (M_DEV, D), 0)
             mesh_v[...] = jnp.where(slot < owned[0], mesh_v[...].astype(F32), 0.0).astype(BF16)
-            outs.append(pltpu.make_async_copy(mesh_v, mesh_out, out_sem.at[tiles]))
+            outs.append(pltpu.make_async_copy(mesh_v, mesh_out, out_sem.at[len(outs)]))
             outs[-1].start()
     for copy in outs:
         copy.wait()
@@ -713,7 +739,6 @@
 def decode_part(*operands):
     vmem = pltpu.VMEM
     anywhere = pl.BlockSpec(memory_space=pl.ANY)
-    tiles = G_DEV // DEC_TILE
     return pl.pallas_call(
         decode_kernel,
         name="decode_part",
@@ -724,9 +749,10 @@
             jax.ShapeDtypeStruct((M_DEV, D), BF16),
         ],
         scratch_shapes=[
-            vmem((3, G_DEV, 384), BF16),
-            vmem((G_DEV, D), BF16),
-            vmem((384, D), BF16),
+            vmem((3, G_DEV, 128), BF16),
+            vmem((8 * HB, D), BF16),
+            vmem((3, G_DEV, D), BF16),
+            vmem((DEC_TILE, D), F32),
             vmem((G_DEV, D), BF16),
             vmem((G_DEV, D), BF16),
             vmem((G_DEV, D), BF16),
@@ -735,8 +761,8 @@
             vmem((D, D), BF16),
             vmem((4, D), F32),
             vmem((4, D), F32),
-            pltpu.SemaphoreType.DMA((8 + 4 * tiles,)),
-            pltpu.SemaphoreType.DMA((tiles + 1,)),
+            pltpu.SemaphoreType.DMA((21,)),
+            pltpu.SemaphoreType.DMA((4,)),
         ],
         compiler_params=pltpu.CompilerParams(vmem_limit_bytes=60 * 1024 * 1024),
     )(*operands)
@@ -762,7 +788,7 @@
     node_bias,
     node_gain,
 ):
-    table, mesh_three, gq, gp, picks, seconds = mesh_part(
+    halo, mesh_three, sums, gp, picks, seconds = mesh_part(
         grid_nodes,
         mesh_nodes,
         grid_rim,
@@ -784,8 +810,8 @@
     grid_out, mesh_out = decode_part(
         owned_nodes,
         picks,
-        table,
-        gq,
+        halo,
+        sums,
         gp,
         grid_nodes,
         mesh_three,

time: 69.2 us -> 67.7 us (0.978)
  Pallas kernels: 67.6 us -> 65.7 us
    pallas_call x1, Pallas kernels: 58.9 us -> 57.9 us  [mesh_part(): pl.pallas_call(mesh_kernel, name='mesh_part', in_specs=[anywhere] * 17, o...]
    pallas_call x1, Pallas kernels: 8.71 us -> 7.84 us  [decode_part(): pl.pallas_call(decode_kernel, name='decode_part', in_specs=[pl.BlockSpec(...]
where the time goes in v4:
time: 67.7 us; the launch traced here: 67.2 us
  Pallas kernels  65.7 us (97%)
  between operations  1.47 us (2%)
    pallas_call x1, Pallas kernels, mesh_part(): pl.pallas_call(mesh_kernel, name='mesh_part', in_specs=[anywhere] * 17, o...  57.9 us
    pallas_call x1, Pallas kernels, decode_part(): pl.pallas_call(decode_kernel, name='decode_part', in_specs=[pl.BlockSpec(...  7.84 us

profile of v4, /device:TPU:0, one launch (start us, length us, event | category | flops | bytes accessed | tf_op | source)
XLA Modules:
  0.0 67.2 jit_solution(10102074519667272547)
XLA Ops:
  1.3 57.9 %mesh_part.1 = (bf16[128,512]{1,0:T(8,128)(2,1)}, bf16[192,512]{1,0:T(8,128)(2,1)}, bf16[3,1024,512]{2,1,0:T(8,128)(2,1)}, bf16[1024,512]{1,0:T(8,128)(2,1)}, bf...) custom-call(bf16[1024,512]{1,0:T(8,128)(2,1)} %grid_rows.1, bf16[192,512]{1,0:T(8,128)(2,1)} %mesh_nodes.1, ...), custom_call_target="tpu_custom_call" | custom-call | tf_op jit(solution)/shard_map/mesh_part/pallas_call | solution.py:555
  59.2 7.8 %decode_part.1 = (bf16[1024,512]{1,0:T(8,128)(2,1)}, bf16[192,512]{1,0:T(8,128)(2,1)}) custom-call(s32[1]{0:T(128)S(6)} %copy.20.owned, bf16[3,1024,128]{2,1,0:T(8,128)(2,1)} %get-tuple-element.8.picks, bf16[128,512]{1,0:T(8,128)(2,1)} %get-tuple-element.9.halo, bf16[3,1024,512]{2,1,0:T(8,128)(2,1)} %get-tuple-element.10.sums, ...), custom_call_target="tpu_custom_call" | custom-call | tf_op jit(solution)/shard_map/decode_part/pallas_call | solution.py:742

commit v5 on v4

--- a/solution.py
+++ b/solution.py
@@ -106,10 +106,19 @@
     return jnp.concatenate(parts, 1)
 
 
-def scatter_matrix(row):
+def receivers(row):
     slots = lax.broadcasted_iota(jnp.int32, (M_DEV, row.shape[1]), 0).astype(F32).astype(BF16)
-    ids = row.astype(F32).astype(BF16)
-    return jnp.where(slots == ids, jnp.ones((), BF16), jnp.zeros((), BF16))
+    return slots == row.astype(F32).astype(BF16)
+
+
+def scatter_matrix(row, values):
+    spread = jnp.mean(values * values, axis=-1, keepdims=True)
+    scale = lax.rsqrt(spread + EPSILON)
+    parts = []
+    for start in range(0, values.shape[0], 128):
+        parts.append(jnp.broadcast_to(scale[start : start + 128], (128, 128)).T[0:1, :])
+    scales = jnp.concatenate(parts, 1).astype(BF16)
+    return jnp.where(receivers(row), scales, jnp.zeros((), BF16))
 
 
 def node_update(rows, totals, first_own, first_sum, bias, second, gain):
@@ -243,7 +252,7 @@
 
     copies = []
     arrived("grim", "grid")
-    for pair in ((5, 4), (3, 2), (7, 6), (1, 0)):
+    for pair in ((5, 4), (7, 6, 3), (2, 1, 0)):
         cols = columns(jnp.concatenate([grim_v[0, k : k + 1, :] for k in pair], 1))
         rows = dot(one_hot(cols, 0, G_DEV), grid_v[...]).astype(BF16)
         if not copies:
@@ -338,14 +347,20 @@
             if step < tiles:
                 half = picked(step * tile)
             if 0 <= step - 2:
-                message = normalised(result.pop(step - 2)).astype(BF16)
+                values = result.pop(step - 2)
+                targets = edges[0, 1:2, (step - 2) * tile : (step - 1) * tile]
+                if section == 0:
+                    scatter = jnp.where(receivers(targets), jnp.ones((), BF16), jnp.zeros((), BF16))
+                    message = normalised(values).astype(BF16)
+                else:
+                    scatter = scatter_matrix(targets, values)
+                    message = values.astype(BF16)
             if 0 <= step - 1 < tiles:
                 result[step - 1] = dot(hidden.pop(step - 1), es_v[section])
             if step < tiles:
                 hidden[step] = silu_of_half(half)
             if 0 <= step - 2:
-                targets = edges[0, 1:2, (step - 2) * tile : (step - 1) * tile]
-                totals[...] += dot(scatter_matrix(targets), message)
+                totals[...] += dot(scatter, message)
 
     def updated(section, rows, sums):
         return node_update(
@@ -392,20 +407,21 @@
             copy.start()
             started.append(copy)
         if first:
-            table[0:first, :] = proj
+            table[0:M_DEV, :] = proj
         return started
 
     arrived("ef1")
-    copies = mesh_halo(1, 8, short_rim, short_table, M_DEV)
-    short_table[M_DEV + 8 * HB : 512, :] = (0.5 * (dot(mesh_v[...], ef_v[1, 1]) + eb_v[1:2, :])).astype(
+    copies = mesh_halo(1, 8, short_rim, short_table, 2 * M_DEV)
+    short_table[M_DEV : 2 * M_DEV, :] = (0.5 * (dot(mesh_v[...], ef_v[1, 1]) + eb_v[1:2, :])).astype(
         BF16
     )
     arrived("short")
 
     def short_picks(step, carry):
         here = pl.ds(pl.multiple_of(step * TILE_LOCAL, TILE_LOCAL), TILE_LOCAL)
-        senders = columns(short_v[0, 0:1, here])
-        targets = columns(short_v[0, 1:2, here] + (M_DEV + 8 * HB))
+        senders = short_v[0, 0:1, here]
+        senders = columns(jnp.where(senders < M_DEV, senders, senders + M_DEV))
+        targets = columns(short_v[0, 1:2, here] + M_DEV)
         picks_v[here, 0:512] = double_one_hot(senders, targets, 512)
         return carry
 
@@ -424,13 +440,18 @@
         list_picks[start : start + 512, :] = one_hot(
             (None, jnp.broadcast_to(col, (512, 128)).astype(BF16)), 0, 128
         )
+    for index in range(E_MESH // TILE_LOCAL):
+        here = tile_of(index)
+        partial[here, :] = dot(picks_v[here, 0:256], short_table[0:256, :]).astype(BF16)
     pl.semaphore_wait(spread_sem.at[1], 8)
     greet(spread_sem.at[2], 0, 4, (3, 4))
     for copy in copies:
         copy.wait()
 
     def short_picked(start):
-        return dot(picks_v[pl.ds(start, TILE_MESH), 0:512], short_table[...]).astype(BF16)
+        here = pl.ds(start, TILE_MESH)
+        late = dot(picks_v[here, 256:512], short_table[256:512, :])
+        return partial[here, :] + late.astype(BF16)
 
     rounds(1, TILE_MESH, short_v, E_MESH, short_picked)
 
@@ -691,14 +712,24 @@
         )
         outs[-1].start()
 
+    def half_sums(step):
+        half, k = order[step]
+        loads["picks", half, k].wait()
+        loads["sums", half, k].wait()
+        picked = dot(picks_v[k, rows_of(half), :], halo_v[...]).astype(BF16)
+        return silu_of_half(picked + sums_v[k, rows_of(half), :])
+
     loads["halo"].wait()
-    for step in range(11):
-        if step < 6:
-            half, k = order[step]
-            loads["picks", half, k].wait()
-            loads["sums", half, k].wait()
-            picked = dot(picks_v[k, rows_of(half), :], halo_v[...]).astype(BF16)
-        if 0 <= step - 2 < 6:
+    count = len(order)
+    for step in range(count + 5):
+        if step < count:
+            hidden[step] = half_sums(step)
+        if step == 1:
+            loads["es"].wait()
+            loads["eg"].wait()
+        if 0 <= step - 1 < count:
+            result[step - 1] = dot(hidden.pop(step - 1), second_v[0])
+        if 0 <= step - 2 < count:
             before, part = order[step - 2]
             message = normalised(result.pop(step - 2))
             if part == 0:
@@ -707,19 +738,12 @@
                 added_v[...] += message
             else:
                 total_v[rows_of(before), :] = ((added_v[...] + message) * eg_v[3:4, :]).astype(BF16)
-        if 0 <= step - 1 < 6:
-            if step == 1:
-                loads["es"].wait()
-                loads["eg"].wait()
-            result[step - 1] = dot(hidden.pop(step - 1), second_v[0])
         if step == 5:
             for name in ("nf", "ns", "ng", "gp", "grid"):
                 loads[name].wait()
         pres = {}
         for block in starts.get(step, ()):
             pres[block] = (0.5 * dot(total_v[pl.ds(*block), :], sum_v[...])).astype(BF16)
-        if step < 6:
-            hidden[step] = silu_of_half(picked + sums_v[k, rows_of(half), :])
         for block in list(update):
             finish(*block)
         for block in list(node):

time: 67.7 us -> 67 us (0.990)
  Pallas kernels: 65.7 us -> 64.8 us
    pallas_call x1, Pallas kernels: 57.9 us -> 57.1 us  [mesh_part(): pl.pallas_call(mesh_kernel, name='mesh_part', in_specs=[anywhere] * 17, o...]
where the time goes in v5:
time: 67 us; the launch traced here: 66.3 us
  Pallas kernels  64.8 us (97%)
  between operations  1.47 us (2%)
    pallas_call x1, Pallas kernels, mesh_part(): pl.pallas_call(mesh_kernel, name='mesh_part', in_specs=[anywhere] * 17, o...  57.1 us
    pallas_call x1, Pallas kernels, decode_part(): pl.pallas_call(decode_kernel, name='decode_part', in_specs=[pl.BlockSpec(...  7.76 us

profile of v5, /device:TPU:0, one launch (start us, length us, event | category | flops | bytes accessed | tf_op | source)
XLA Modules:
  0.0 66.3 jit_solution(11304722183107401611)
XLA Ops:
  1.3 57.1 %mesh_part.1 = (bf16[128,512]{1,0:T(8,128)(2,1)}, bf16[192,512]{1,0:T(8,128)(2,1)}, bf16[3,1024,512]{2,1,0:T(8,128)(2,1)}, bf16[1024,512]{1,0:T(8,128)(2,1)}, bf...) custom-call(bf16[1024,512]{1,0:T(8,128)(2,1)} %grid_rows.1, bf16[192,512]{1,0:T(8,128)(2,1)} %mesh_nodes.1, ...), custom_call_target="tpu_custom_call" | custom-call | tf_op jit(solution)/shard_map/mesh_part/pallas_call | solution.py:576
  58.3 7.8 %decode_part.1 = (bf16[1024,512]{1,0:T(8,128)(2,1)}, bf16[192,512]{1,0:T(8,128)(2,1)}) custom-call(s32[1]{0:T(128)S(6)} %copy.20.owned, bf16[3,1024,128]{2,1,0:T(8,128)(2,1)} %get-tuple-element.8.picks, bf16[128,512]{1,0:T(8,128)(2,1)} %get-tuple-element.9.halo, bf16[3,1024,512]{2,1,0:T(8,128)(2,1)} %get-tuple-element.10.sums, ...), custom_call_target="tpu_custom_call" | custom-call | tf_op jit(solution)/shard_map/decode_part/pallas_call | solution.py:766

commit v6 on v5

--- a/solution.py
+++ b/solution.py
@@ -60,6 +60,11 @@
     return centred * lax.rsqrt(spread + EPSILON)
 
 
+def normalised_bf16(centred):
+    spread = jnp.mean(centred * centred, axis=-1, keepdims=True)
+    return centred.astype(BF16) * lax.rsqrt(spread + EPSILON).astype(BF16)
+
+
 def spread_out(row):
     parts = []
     for start in range(0, row.shape[1], 128):
@@ -109,16 +114,6 @@
 def receivers(row):
     slots = lax.broadcasted_iota(jnp.int32, (M_DEV, row.shape[1]), 0).astype(F32).astype(BF16)
     return slots == row.astype(F32).astype(BF16)
-
-
-def scatter_matrix(row, values):
-    spread = jnp.mean(values * values, axis=-1, keepdims=True)
-    scale = lax.rsqrt(spread + EPSILON)
-    parts = []
-    for start in range(0, values.shape[0], 128):
-        parts.append(jnp.broadcast_to(scale[start : start + 128], (128, 128)).T[0:1, :])
-    scales = jnp.concatenate(parts, 1).astype(BF16)
-    return jnp.where(receivers(row), scales, jnp.zeros((), BF16))
 
 
 def node_update(rows, totals, first_own, first_sum, bias, second, gain):
@@ -349,12 +344,11 @@
             if 0 <= step - 2:
                 values = result.pop(step - 2)
                 targets = edges[0, 1:2, (step - 2) * tile : (step - 1) * tile]
+                scatter = jnp.where(receivers(targets), jnp.ones((), BF16), jnp.zeros((), BF16))
                 if section == 0:
-                    scatter = jnp.where(receivers(targets), jnp.ones((), BF16), jnp.zeros((), BF16))
                     message = normalised(values).astype(BF16)
                 else:
-                    scatter = scatter_matrix(targets, values)
-                    message = values.astype(BF16)
+                    message = normalised_bf16(values)
             if 0 <= step - 1 < tiles:
                 result[step - 1] = dot(hidden.pop(step - 1), es_v[section])
             if step < tiles:
@@ -705,8 +699,8 @@
 
     def finish(first, count):
         here = pl.ds(first, count)
-        rows = grid_v[here, :].astype(F32) + normalised(update.pop((first, count))) * ng_v[3:4, :]
-        grid_v[here, :] = rows.astype(BF16)
+        change = normalised_bf16(update.pop((first, count))) * ng_v[3:4, :].astype(BF16)
+        grid_v[here, :] = grid_v[here, :] + change
         outs.append(
             pltpu.make_async_copy(grid_v.at[here], grid_out.at[here], out_sem.at[len(outs)])
         )
@@ -731,13 +725,13 @@
             result[step - 1] = dot(hidden.pop(step - 1), second_v[0])
         if 0 <= step - 2 < count:
             before, part = order[step - 2]
-            message = normalised(result.pop(step - 2))
+            message = normalised_bf16(result.pop(step - 2))
             if part == 0:
                 added_v[...] = message
             elif part == 1:
                 added_v[...] += message
             else:
-                total_v[rows_of(before), :] = ((added_v[...] + message) * eg_v[3:4, :]).astype(BF16)
+                total_v[rows_of(before), :] = (added_v[...] + message) * eg_v[3:4, :].astype(BF16)
         if step == 5:
             for name in ("nf", "ns", "ng", "gp", "grid"):
                 loads[name].wait()
@@ -776,7 +770,7 @@
             vmem((3, G_DEV, 128), BF16),
             vmem((8 * HB, D), BF16),
             vmem((3, G_DEV, D), BF16),
-            vmem((DEC_TILE, D), F32),
+            vmem((DEC_TILE, D), BF16),
             vmem((G_DEV, D), BF16),
             vmem((G_DEV, D), BF16),
             vmem((G_DEV, D), BF16),

time: 67 us -> 66.9 us (level)
  no operation moved by 1% of the time
where the time goes in v6:
time: 66.9 us; the launch traced here: 66.1 us
  Pallas kernels  64.6 us (97%)
  between operations  1.47 us (2%)
    pallas_call x1, Pallas kernels, mesh_part(): pl.pallas_call(mesh_kernel, name='mesh_part', in_specs=[anywhere] * 17, o...  57 us
    pallas_call x1, Pallas kernels, decode_part(): pl.pallas_call(decode_kernel, name='decode_part', in_specs=[pl.BlockSpec(...  7.63 us

profile of v6, /device:TPU:0, one launch (start us, length us, event | category | flops | bytes accessed | tf_op | source)
XLA Modules:
  0.0 66.1 jit_solution(9948924765315259917)
XLA Ops:
  1.3 57.0 %mesh_part.1 = (bf16[128,512]{1,0:T(8,128)(2,1)}, bf16[192,512]{1,0:T(8,128)(2,1)}, bf16[3,1024,512]{2,1,0:T(8,128)(2,1)}, bf16[1024,512]{1,0:T(8,128)(2,1)}, bf...) custom-call(bf16[1024,512]{1,0:T(8,128)(2,1)} %grid_rows.1, bf16[192,512]{1,0:T(8,128)(2,1)} %mesh_nodes.1, ...), custom_call_target="tpu_custom_call" | custom-call | tf_op jit(solution)/shard_map/mesh_part/pallas_call | solution.py:570
  58.3 7.6 %decode_part.1 = (bf16[1024,512]{1,0:T(8,128)(2,1)}, bf16[192,512]{1,0:T(8,128)(2,1)}) custom-call(s32[1]{0:T(128)S(6)} %copy.20.owned, bf16[3,1024,128]{2,1,0:T(8,128)(2,1)} %get-tuple-element.8.picks, bf16[128,512]{1,0:T(8,128)(2,1)} %get-tuple-element.9.halo, bf16[3,1024,512]{2,1,0:T(8,128)(2,1)} %get-tuple-element.10.sums, ...), custom_call_target="tpu_custom_call" | custom-call | tf_op jit(solution)/shard_map/decode_part/pallas_call | solution.py:760

commit v7 on v6

--- a/solution.py
+++ b/solution.py
@@ -14,7 +14,7 @@
 KL = 8
 CS = 16
 NOWHERE = 4095
-EARLY = 4
+EARLY = 6
 N_AA = 8
 N_BA = 16
 DEVICES = 128
@@ -247,7 +247,7 @@
 
     copies = []
     arrived("grim", "grid")
-    for pair in ((5, 4), (7, 6, 3), (2, 1, 0)):
+    for pair in ((5, 4), (7, 3, 2), (6, 1, 0)):
         cols = columns(jnp.concatenate([grim_v[0, k : k + 1, :] for k in pair], 1))
         rows = dot(one_hot(cols, 0, G_DEV), grid_v[...]).astype(BF16)
         if not copies:

time: 66.9 us -> 68.5 us (1.024)
  Pallas kernels: 64.6 us -> 66.5 us
    pallas_call x1, Pallas kernels: 57 us -> 58.9 us  [mesh_part(): pl.pallas_call(mesh_kernel, name='mesh_part', in_specs=[anywhere] * 17, o...]
where the time goes in v7:
time: 68.5 us; the launch traced here: 68 us
  Pallas kernels  66.5 us (97%)
  between operations  1.47 us (2%)
    pallas_call x1, Pallas kernels, mesh_part(): pl.pallas_call(mesh_kernel, name='mesh_part', in_specs=[anywhere] * 17, o...  58.9 us
    pallas_call x1, Pallas kernels, decode_part(): pl.pallas_call(decode_kernel, name='decode_part', in_specs=[pl.BlockSpec(...  7.65 us

profile of v7, /device:TPU:0, one launch (start us, length us, event | category | flops | bytes accessed | tf_op | source)
XLA Modules:
  0.0 68.0 jit_solution(7652759211674300953)
XLA Ops:
  1.3 58.9 %mesh_part.1 = (bf16[128,512]{1,0:T(8,128)(2,1)}, bf16[192,512]{1,0:T(8,128)(2,1)}, bf16[3,1024,512]{2,1,0:T(8,128)(2,1)}, bf16[1024,512]{1,0:T(8,128)(2,1)}, bf...) custom-call(bf16[1024,512]{1,0:T(8,128)(2,1)} %grid_rows.1, bf16[192,512]{1,0:T(8,128)(2,1)} %mesh_nodes.1, ...), custom_call_target="tpu_custom_call" | custom-call | tf_op jit(solution)/shard_map/mesh_part/pallas_call | solution.py:570
  60.2 7.6 %decode_part.1 = (bf16[1024,512]{1,0:T(8,128)(2,1)}, bf16[192,512]{1,0:T(8,128)(2,1)}) custom-call(s32[1]{0:T(128)S(6)} %copy.20.owned, bf16[3,1024,128]{2,1,0:T(8,128)(2,1)} %get-tuple-element.8.picks, bf16[128,512]{1,0:T(8,128)(2,1)} %get-tuple-element.9.halo, bf16[3,1024,512]{2,1,0:T(8,128)(2,1)} %get-tuple-element.10.sums, ...), custom_call_target="tpu_custom_call" | custom-call | tf_op jit(solution)/shard_map/decode_part/pallas_call | solution.py:760
